TPU v7x, 128 devices: a whole 4x4x4 slice. The times are simulated.
128 devices in a mesh: layer: 32 (over x_hi, y, z), dir: 4 (over x_lo, core).
Axes of the slice: x: 4 (x_hi: 2, x_lo: 2; x = x_hi * 2 + x_lo), y: 4, z: 4, core: 2. Of those that a mesh axis runs over, the one named last changes fastest.
Arguments:
- screens: bfloat16 [3, 2048, 16384], P(None, 'dir', 'layer'), may hold values from -6 to 6
- amplitude: float32 [1024, 1280], P('layer'), may hold values from 0.5 to 2
- wind: int32 [3, 2], replicated, may hold values from -8 to 8, as said below
- offsets: int32 [4, 3, 2], replicated, may hold values from 0 to 16383, as said below
- ratio: int32 [4, 3, 2], replicated, may hold values from 64 to 192, as said below
Outputs:
- new_screens: bfloat16 [3, 2048, 16384], P(None, 'dir', 'layer')
- spots: float32 [4, 2048, 2560], P('dir', 'layer')
Inputs may be any that keep to these rules, and one draw needn't show every extreme that they name: wind[l, 0] is layer l's row shift and wind[l, 1] its column shift; no shift is zero; one layer has column shift +8 and a row shift above zero, another has column shift -8 and a row shift below zero. offsets[d, l, 0] is a screen row below 2048, offsets[d, l, 1] a screen column below 16384. ratio[d, l] = (num, den) with 64 <= den <= 128 and den <= num <= den + den // 2; some entry is (192, 128) and another (64, 64).
All inputs are finite; a program needn't handle non-finite values.
Results may differ from a plain program's by a relative error of at most 0.009.
Values may be sent and summed in bfloat16 or wider, within the bound.
A program may use at most 64 MiB of HBM per device.

v0:
```python
import jax
import jax.numpy as jnp
from jax import lax
from jax.sharding import PartitionSpec as P

SUB_PIX = 16
SPOT_PIX = 32
WIND_MAX = 8


def with_halo(shard, sides, width):
    for axis, dim in sides:
        peers, length = (lax.axis_size(axis), shard.shape[dim])
        up = [(i, (i + 1) % peers) for i in range(peers)]
        down = [(j, i) for i, j in up]
        last = lax.slice_in_dim(shard, length - width, length, axis=dim)
        initial = lax.slice_in_dim(shard, 0, width, axis=dim)
        before = lax.ppermute(last, axis, up)
        after = lax.ppermute(initial, axis, down)
        shard = jnp.concatenate([before, shard, after], axis=dim)
    return shard


def spans(anchor, stretch_num, stretch_den, count, length):
    pixel = jnp.arange(count, dtype=jnp.int32)
    stretched = pixel * stretch_num
    base = (anchor + stretched // stretch_den) % length
    upper = (base + 1) % length
    fraction = (stretched % stretch_den).astype(jnp.float32) / stretch_den.astype(jnp.float32)
    return (base, upper, (1.0 - fraction).astype(jnp.bfloat16), fraction.astype(jnp.bfloat16))


def weights_rows(anchor, stretch_num, stretch_den, count, length, width):
    base, upper, low_weight, high_weight = spans(anchor, stretch_num, stretch_den, count, length)
    index = jnp.arange(width, dtype=jnp.int32)
    matrix = jnp.where(
        index[None, :] == base[:, None], low_weight[:, None], jnp.zeros((), jnp.bfloat16)
    )
    return jnp.where(index[None, :] == upper[:, None], high_weight[:, None], matrix)


def weights_cols(anchor, stretch_num, stretch_den, count, length, start, width):
    base, upper, low_weight, high_weight = spans(anchor, stretch_num, stretch_den, count, length)
    index = start + jnp.arange(width, dtype=jnp.int32)
    matrix = jnp.where(
        index[:, None] == base[None, :], low_weight[None, :], jnp.zeros((), jnp.bfloat16)
    )
    return jnp.where(index[:, None] == upper[None, :], high_weight[None, :], matrix)


def dft_tables():
    freq = jnp.arange(SPOT_PIX, dtype=jnp.int32)[:, None] - SPOT_PIX // 2
    pixel = jnp.arange(SUB_PIX, dtype=jnp.int32)[None, :]
    turns = freq * pixel % SPOT_PIX
    angle = turns.astype(jnp.float32) * (2.0 * jnp.pi / SPOT_PIX)
    return (jnp.cos(angle), -jnp.sin(angle))


def imaging(phase, amplitude):
    rows, cols = phase.shape
    sub_rows = rows // SUB_PIX
    sub_cols = cols // SUB_PIX
    real = (amplitude * jnp.cos(phase)).reshape(sub_rows, SUB_PIX, sub_cols, SUB_PIX)
    imag = (amplitude * jnp.sin(phase)).reshape(sub_rows, SUB_PIX, sub_cols, SUB_PIX)
    cos_table, sin_table = dft_tables()
    highest = lax.Precision.HIGHEST
    half_real = jnp.einsum("aibj,kj->aibk", real, cos_table, precision=highest) - jnp.einsum(
        "aibj,kj->aibk", imag, sin_table, precision=highest
    )
    half_imag = jnp.einsum("aibj,kj->aibk", real, sin_table, precision=highest) + jnp.einsum(
        "aibj,kj->aibk", imag, cos_table, precision=highest
    )
    full_real = jnp.einsum("ki,aibl->akbl", cos_table, half_real, precision=highest) - jnp.einsum(
        "ki,aibl->akbl", sin_table, half_imag, precision=highest
    )
    full_imag = jnp.einsum("ki,aibl->akbl", cos_table, half_imag, precision=highest) + jnp.einsum(
        "ki,aibl->akbl", sin_table, half_real, precision=highest
    )
    intensity = full_real * full_real + full_imag * full_imag
    totals = jnp.sum(intensity, axis=(1, 3), keepdims=True)
    normed = intensity * float(SPOT_PIX * SPOT_PIX) / totals
    return normed.reshape(sub_rows * SPOT_PIX, sub_cols * SPOT_PIX)


def per_device(screens, amplitude, wind, offsets, ratio):
    layers, rows_dev, cols_dev = screens.shape
    n_layer = lax.axis_size("layer")
    n_dir = lax.axis_size("dir")
    screen_rows = rows_dev * n_dir
    screen_cols = cols_dev * n_layer
    pupil_rows = amplitude.shape[0] * n_layer
    pupil_cols = amplitude.shape[1]
    direction = lax.axis_index("dir")
    column_start = lax.axis_index("layer") * cols_dev
    widened = with_halo(screens, (("layer", 2), ("dir", 1)), WIND_MAX)
    moved = []
    for level in range(layers):
        corner = (jnp.int32(WIND_MAX) - wind[level, 0], jnp.int32(WIND_MAX) - wind[level, 1])
        moved.append(lax.dynamic_slice(widened[level], corner, (rows_dev, cols_dev)))
    new_screens = jnp.stack(moved)
    piece = lax.all_gather(new_screens, "dir", axis=1, tiled=True)
    sums = []
    for add_level in range(layers):
        weights = weights_rows(
            offsets[direction, add_level, 0],
            ratio[direction, add_level, 0],
            ratio[direction, add_level, 1],
            pupil_rows,
            screen_rows,
            piece.shape[1],
        )
        sums.append(jnp.dot(weights, piece[add_level], preferred_element_type=jnp.float32))
    projected = jnp.stack(sums).astype(jnp.bfloat16)
    col_weights = [
        weights_cols(
            offsets[direction, level, 1],
            ratio[direction, level, 0],
            ratio[direction, level, 1],
            pupil_cols,
            screen_cols,
            column_start,
            cols_dev,
        )
        for level in range(layers)
    ]
    total = jnp.zeros((pupil_rows // n_layer * lax.axis_size("layer"), pupil_cols), jnp.float32)
    for level in range(layers):
        total = total + jnp.dot(
            projected[level], col_weights[level], preferred_element_type=jnp.float32
        )
    phase = lax.psum_scatter(
        total.astype(jnp.bfloat16), "layer", scatter_dimension=0, tiled=True
    ).astype(jnp.float32)
    spots = imaging(phase, amplitude)[None]
    return (new_screens, spots)


def solution(mesh):
    return jax.shard_map(
        per_device,
        mesh=mesh,
        in_specs=(P(None, "dir", "layer"), P("layer", None), P(), P(), P()),
        out_specs=(P(None, "dir", "layer"), P("dir", "layer", None)),
        check_vma=False,
    )
```

profile of v0, /device:TPU:0, one launch (start us, length us, event | category | flops | bytes accessed | tf_op | source)
XLA Modules:
  0.0 353.0 jit_solution(13287869215477032080)
XLA Ops:
  8.6 2.1 collective-permute-start
  10.7 7.1 %collective-permute-start.1 = (bf16[3,512,8]{2,1,0:T(8,128)(2,1)S(1)}, bf16[3,512,8]{2,1,0:T(8,128)(2,1)S(1)}, u32[]{:S(2)}, u32[]{:S(2)}) collective-permute-start(bf16[3,512,8]{2,1,0:T(8,128)(2,1)S(1)} %get-tuple-element.8), channel_id=1, source_target_pairs={{4,0},{8,4},{12,8},{16,12},{20,16},{24,20},{28,24},{32,28},{36,32}... | collective-permute-start | bytes 73736 | tf_op jit(solution)/shard_map/ppermute | solution.py:19
  17.8 9.0 %collective-permute-done = bf16[3,512,8]{2,1,0:T(8,128)(2,1)S(1)} collective-permute-done((bf16[3,512,8]{2,1,0:T(8,128)(2,1)S(1)}, bf16[3,512,8]{2,1,0:T(8,128)(2,1)S(1)}, u32[]{:S(2)}, u32[]{:S(2)}) %collective-permute-start) | collective-permute-done | bytes 24608 | tf_op jit(solution)/shard_map/ppermute | solution.py:18
  27.0 1.7 collective-permute-start.3
  50.0 1.4 subtract_convert_fusion.3
  56.3 2.0 add_select_fusion.18
  58.4 2.0 add_select_fusion.22
  60.4 2.0 add_select_fusion.14
  62.4 2.1 add_select_fusion.6
  64.4 2.0 add_select_fusion.10
  66.5 2.0 add_select_fusion.2
  68.4 36.3 %all-gather.2.cloned.1.call-done = bf16[3,2048,512]{2,1,0:T(8,128)(2,1)} async-done(((bf16[3,512,512]{2,1,0:T(8,128)(2,1)}), bf16[3,2048,512]{2,1,0:T(8,128)(2,1)}) %all-gather.2.cloned.1.call-update) | async-done | bytes 6291472 | tf_op jit(solution)/shard_map/all_gather | solution.py:101
  104.7 8.1 %fusion.37 = f32[1024,1280]{1,0:T(8,128)} fusion(bf16[3,2048,512]{2,1,0:T(8,128)(2,1)} %all-gather.2.cloned.1.call-done, s32[1024]{0:T(1024)S(1)} %get-tuple-element.36, s32[1024]{0:T(1024)S(1)} %get-tuple-element.35, bf16[1024]{0:T(1024)(128)(2,1)S(1)} %get-tuple-element.40, bf16[1024]{0:T(1024)(128)(2,1)S(1)} %get-tuple-element.43, ...), kind=kOutput, calls=%fused_computation.45 | convolution fusion | flops 3501195264 | bytes 7369728 | tf_op jit(solution)/shard_map/dot_general | solution.py:128
  112.8 8.2 %fusion.40 = f32[1024,1280]{1,0:T(8,128)} fusion(bf16[3,2048,512]{2,1,0:T(8,128)(2,1)} %all-gather.2.cloned.1.call-done, s32[1024]{0:T(1024)S(1)} %get-tuple-element.38, s32[1024]{0:T(1024)S(1)} %get-tuple-element.37, bf16[1024]{0:T(1024)(128)(2,1)S(1)} %get-tuple-element.41, bf16[1024]{0:T(1024)(128)(2,1)S(1)} %get-tuple-element.44, ...), kind=kOutput, calls=%fused_computation.46 | convolution fusion | flops 3501195264 | bytes 7369728 | tf_op jit(solution)/shard_map/dot_general | solution.py:128
  120.9 9.2 %add_convert_fusion = bf16[1024,1280]{1,0:T(8,128)(2,1)} fusion(f32[1024,1280]{1,0:T(8,128)} %fusion.40, f32[1024,1280]{1,0:T(8,128)} %fusion.37, bf16[3,2048,512]{2,1,0:T(8,128)(2,1)} %all-gather.2.cloned.1.call-done, s32[1024]{0:T(1024)S(1)} %get-tuple-element.34, s32[1024]{0:T(1024)S(1)} %get-tuple-element.33, ...), kind=kOutput, calls=%fused_computation.12 | convolution fusion | flops 3505127424 | bytes 15234048 | tf_op jit(solution)/shard_map/dot_general | solution.py:128
  130.1 190.8 %reduce-scatter.2.cloned.1.call-done = bf16[32,1280]{1,0:T(8,128)(2,1)} async-done(((bf16[1024,1280]{1,0:T(8,128)(2,1)}), bf16[32,1280]{1,0:T(8,128)(2,1)}) %reduce-scatter.2.cloned.1.call-update) | async-done | bytes 81936 | tf_op jit(solution)/shard_map/reduce_scatter | solution.py:131
  320.9 1.5 fusion.73
  322.8 3.2 fusion.99
  326.0 3.2 fusion.95
  329.6 3.2 convolution_add_fusion.1
  334.1 3.2 convolution_subtract_fusion.1
  339.8 1.4 fusion.212
  342.4 1.9 copy.23
  344.4 1.8 broadcast_in_dim_reshape.3
  (41 shorter events, 18.2 us)
Async XLA Ops:
  7.2 19.7 %copy-start = (bf16[3,512,512]{2,1,0:T(8,128)(2,1)S(1)}, bf16[3,512,512]{2,1,0:T(8,128)(2,1)}, u32[]{:S(2)}) copy-start(bf16[3,512,512]{2,1,0:T(8,128)(2,1)} %param.5) | copy-start | bytes 4718596
  7.2 21.6 %copy-start.2 = (s32[3,2]{0,1:T(2,128)S(1)}, s32[3,2]{0,1:T(2,128)}, u32[]{:S(2)}) copy-start(s32[3,2]{0,1:T(2,128)} %param.7) | copy-start | bytes 76
  7.2 97.5 %all-gather.2.cloned.1.call-start = ((), (), s32[]{:S(2)}) async-start(), calls=%async_computation.1 | async-start | bytes 7864320 | tf_op jit(solution)/shard_map/all_gather | solution.py:101
  8.6 18.2 %collective-permute-start = (bf16[3,512,8]{2,1,0:T(8,128)(2,1)S(1)}, bf16[3,512,8]{2,1,0:T(8,128)(2,1)S(1)}, u32[]{:S(2)}, u32[]{:S(2)}) collective-permute-start(bf16[3,512,8]{2,1,0:T(8,128)(2,1)S(1)} %get-tuple-element.7), channel_id=1, source_target_pairs={{0,4},{4,8},{8,12},{12,16},{16,20},{20,24},{24,28},{28,32},{32,36}... | collective-permute-start | bytes 73736 | tf_op jit(solution)/shard_map/ppermute | solution.py:18
  10.7 16.1 %collective-permute-start.1 = (bf16[3,512,8]{2,1,0:T(8,128)(2,1)S(1)}, bf16[3,512,8]{2,1,0:T(8,128)(2,1)S(1)}, u32[]{:S(2)}, u32[]{:S(2)}) collective-permute-start(bf16[3,512,8]{2,1,0:T(8,128)(2,1)S(1)} %get-tuple-element.8), channel_id=1, source_target_pairs={{4,0},{8,4},{12,8},{16,12},{20,16},{24,20},{28,24},{32,28},{36,32}... | collective-permute-start | bytes 73736 | tf_op jit(solution)/shard_map/ppermute | solution.py:19
  27.0 10.1 %collective-permute-start.2 = (bf16[3,8,528]{2,1,0:T(8,128)(2,1)S(1)}, bf16[3,8,528]{2,1,0:T(8,128)(2,1)S(1)}, u32[]{:S(2)}, u32[]{:S(2)}) collective-permute-start(bf16[3,8,528]{2,1,0:T(8,128)(2,1)S(1)} %get-tuple-element.2), channel_id=1, source_target_pairs={{0,1},{1,2},{2,3},{3,0},{4,5},{5,6},{6,7},{7,4},{8,9},{9,10},{10,1... | collective-permute-start | bytes 76040 | tf_op jit(solution)/shard_map/ppermute | solution.py:18
  27.0 10.0 %collective-permute-start.3 = (bf16[3,8,528]{2,1,0:T(8,128)(2,1)S(1)}, bf16[3,8,528]{2,1,0:T(8,128)(2,1)S(1)}, u32[]{:S(2)}, u32[]{:S(2)}) collective-permute-start(bf16[3,8,528]{2,1,0:T(8,128)(2,1)S(1)} %get-tuple-element.3), channel_id=1, source_target_pairs={{1,0},{2,1},{3,2},{0,3},{5,4},{6,5},{7,6},{4,7},{9,8},{10,9},{11,1... | collective-permute-start | bytes 76040 | tf_op jit(solution)/shard_map/ppermute | solution.py:19
  39.3 1.6 copy-start.3
  39.3 10.0 %copy-start.4 = (s32[4,3,2]{0,2,1:T(2,128)S(1)}, s32[4,3,2]{0,2,1:T(2,128)}, u32[]{:S(2)}) copy-start(s32[4,3,2]{0,2,1:T(2,128)} %param.8) | copy-start | bytes 292
  40.7 280.2 %reduce-scatter.2.cloned.1.call-start = ((), (), s32[]{:S(2)}) async-start(), calls=%async_computation.2 | async-start | bytes 2703360 | tf_op jit(solution)/shard_map/reduce_scatter | solution.py:131
  130.1 190.8 %copy-start.1 = (f32[32,1280]{1,0:T(8,128)S(1)}, f32[32,1280]{1,0:T(8,128)}, u32[]{:S(2)}) copy-start(f32[32,1280]{1,0:T(8,128)} %param.6) | copy-start | bytes 491524
Sparse Core Ops, SparseCore 0:
  40.8 63.8 all-gather.1
  130.2 190.6 reduce-scatter.1
where the time goes:
time: 354 us; the launch traced here: 353 us
  waiting for transfers between devices  236 us (67%)
  matrix products  43.4 us (12%)
  between operations  29.6 us (8%)
  other arithmetic  23.6 us (7%)
  starting transfers between devices  11.2 us (3%)
  local copies, waits for them, and re-layouts  9.16 us (3%)
    reduce_scatter x1, waiting for transfers between devices, per_device(): lax.psum_scatter(total.astype(jnp.bfloat16), 'layer', scatter_dimension=0...  191 us
    all_gather x1, waiting for transfers between devices, per_device(): piece = lax.all_gather(new_screens, 'dir', axis=1, tiled=True)  36.3 us
    dot_general x3, matrix products, per_device(): jnp.dot(projected[level], col_weights[level], preferred_element_type=jnp....  25.4 us
    select_n x6, other arithmetic, spans(): upper = (base + 1) % length  12.1 us
    ppermute x2, waiting for transfers between devices, with_halo(): before = lax.ppermute(last, axis, up)  9.03 us
    ppermute x2, starting transfers between devices, with_halo(): after = lax.ppermute(initial, axis, down)  8.84 us
  transfers between devices with their start and end apart: 6, of which 3 were waited for; matrix products, arithmetic and copies ran while one was open for 6% of the time, Pallas kernels for 0%

commit v1 on v0

v1 whole, which is shorter than its diff:
```python
import functools

import jax
import jax.numpy as jnp
import numpy as np
from jax import lax
from jax.experimental import pallas as pl
from jax.experimental.pallas import tpu as pltpu
from jax.sharding import PartitionSpec as P

MESH = pl.DeviceIdType.MESH
SUB = 16
SPOT = 32
HALO = 8
LAYERS = 3
DIRS = 4
ROWS, COLS = 2048, 16384
PR, PC = 1024, 1280
BLK = 512
CHIPS = 64
JT = PC // 128
NPR = 32
F32, BF16, I32 = jnp.float32, jnp.bfloat16, jnp.int32
HIGHEST = lax.Precision.HIGHEST


def iota(shape, dim):
    return lax.broadcasted_iota(I32, shape, dim)


def floor_div(a, den):
    q = jnp.floor(a / den)
    r = a - q * den
    q = q + jnp.where(r >= den, 1.0, 0.0) - jnp.where(r < 0.0, 1.0, 0.0)
    return q


def reciprocals():
    den = np.maximum(np.arange(129), 1)
    return (2 ** 21 // den + 1).astype(np.int32)


def stretch(i, unit, num, den, mul):
    part = i * (num - den)
    whole = (part * mul) >> 21
    rest = part - whole * den
    return unit * (i + whole) + ((unit * rest * mul) >> 21)


def sincos(x):
    n = jnp.floor(x * np.float32(2.0 / np.pi) + 0.5)
    r = x - n * np.float32(1.5703125)
    r = r - n * np.float32(4.837512969970703125e-4)
    r = r - n * np.float32(7.54978995489188216e-8)
    r2 = r * r
    s = r + r * r2 * (
        np.float32(-1.6666654611e-1)
        + r2 * (np.float32(8.3321608736e-3) + r2 * np.float32(-1.9515295891e-4))
    )
    c = (
        1.0
        - 0.5 * r2
        + r2 * r2 * (
            np.float32(4.166664568298827e-2)
            + r2 * (np.float32(-1.388731625493765e-3) + r2 * np.float32(2.443315711809948e-5))
        )
    )
    k = n.astype(I32)
    swap = (k & 1) == 1
    sin = jnp.where(swap, c, s)
    cos = jnp.where(swap, s, c)
    sin = jnp.where((k & 2) == 2, -sin, sin)
    cos = jnp.where(((k + 1) & 2) == 2, -cos, cos)
    return sin, cos


def dft_tables():
    turns = ((np.arange(SPOT)[:, None] - SPOT // 2) * np.arange(SUB)[None, :]) % SPOT
    angle = turns * (2.0 * np.pi / SPOT)
    c, s = np.cos(angle), -np.sin(angle)
    cols = np.concatenate([np.kron(np.eye(8), c.T), np.kron(np.eye(8), s.T)], axis=1)
    cb, sb = np.kron(np.eye(2), c), np.kron(np.eye(2), s)
    rows = np.block([[cb, -sb], [sb, cb]])
    return cols.astype(np.float32), rows.astype(np.float32)


def shift_at(x, k):
    b, xl = x
    px = ((b // 16) * 2 + xl + k % 4) % 4
    py = ((b // 4) % 4 + (k // 4) % 4) % 4
    pz = (b % 4 + k // 16) % 4
    return (px // 2) * 16 + py * 4 + pz, px % 2


def kernel(
    wind, offs, ratio, magic, screens, amp, dcol, drow,
    new_out, spots,
    x, send1, recv_a, recv_b, recv_c, halo_s, halo_r, edge_s, edge_r, y,
    relb, frac, d_buf, e_buf, stage, send2, recv2, wrow, wbig, ampn, field,
    in_sem, s1, r1, hs, hr, es, er, ws, wr, s2, r2, osem, round2,
):
    recv1 = (recv_a, recv_b, recv_c)
    b = lax.axis_index("layer")
    q = lax.axis_index("dir")
    xl, c = q // 2, q % 2
    chip = b * 2 + xl

    def device(pb, pxl):
        return (pb, pxl * 2 + c)

    bar = pltpu.get_barrier_semaphore()

    up = (b, (q + 1) % 4)
    down = (b, (q + 3) % 4)
    right = ((b + 1) % 32, q)
    left = ((b + 31) % 32, q)

    loads = [pltpu.make_async_copy(screens.at[l], x.at[l], in_sem.at[l]) for l in range(LAYERS)]
    for load in loads:
        load.start()
    for dev in (up, down):
        pl.semaphore_signal(bar, inc=1, device_id=dev, device_id_type=MESH)

    def greet(k, _):
        pl.semaphore_signal(bar, inc=1, device_id=device(*group(b, xl, k, 0)), device_id_type=MESH)
        pl.semaphore_signal(bar, inc=1, device_id=device(*group(b, xl, k, 1)), device_id_type=MESH)
        return 0

    lax.fori_loop(1, 8, greet, 0)

    ro, ri = iota((BLK, BLK), 0), iota((BLK, BLK), 1)
    perm = jnp.where(ri == (ro & 7) * 64 + (ro >> 3), 1.0, 0.0).astype(BF16)

    pl.semaphore_wait(bar, 16)

    def greet2(k, _):
        pl.semaphore_signal(round2, inc=1, device_id=device(*group(b, xl, k, 1)), device_id_type=MESH)
        return 0

    lax.fori_loop(1, 8, greet2, 0)

    def permute(l):
        loads[l].wait()
        rows = jnp.dot(perm, x[l], preferred_element_type=F32)
        for t in range(4):
            send1[l, :, t] = rows[:, t * 128:(t + 1) * 128].reshape(CHIPS, 8, 128).astype(BF16)

    def exchange(l):
        def go(k, _):
            pb, pxl = shift_at((b, xl), k)
            pltpu.make_async_remote_copy(
                src_ref=send1.at[l, pb * 2 + pxl],
                dst_ref=recv1[l].at[xl, pl.ds(b * 4, 4)],
                send_sem=s1.at[l], recv_sem=r1.at[l],
                device_id=device(pb, pxl), device_id_type=MESH,
            ).start()
            return 0

        lax.fori_loop(1, CHIPS, go, 0)
        pltpu.make_async_copy(send1.at[l, chip], recv1[l].at[xl, pl.ds(b * 4, 4)], r1.at[l]).start()

    permute(0)
    pl.semaphore_wait(round2, 7)
    exchange(0)
    permute(1)
    exchange(1)
    permute(2)
    exchange(2)

    pick = (iota((8, 128), 0), iota((8, 128), 1))
    first = jnp.where(pick[1] == pick[0], 1.0, 0.0).astype(BF16)
    last = jnp.where(pick[1] == pick[0] + 120, 1.0, 0.0).astype(BF16)
    nt = (((1,), (1,)), ((), ()))
    for l in range(LAYERS):
        halo_s[0, l] = lax.dot_general(
            last, x[l, :, BLK - 128:], nt, preferred_element_type=F32).astype(BF16)
        halo_s[1, l] = lax.dot_general(
            first, x[l, :, :128], nt, preferred_element_type=F32).astype(BF16)
    halos = [
        pltpu.make_async_remote_copy(
            src_ref=halo_s.at[i], dst_ref=halo_r.at[i], send_sem=hs.at[i], recv_sem=hr.at[i],
            device_id=dev, device_id_type=MESH)
        for i, dev in enumerate((right, left))
    ]
    for h in halos:
        h.start()

    px0 = (iota((16, 128), 0) * 128).astype(F32)
    px = px0 + iota((16, 128), 1).astype(F32)
    for d in range(DIRS):
        for l in range(LAYERS):
            num = ratio[d, l, 0].astype(F32)
            den = ratio[d, l, 1].astype(F32)
            start = (offs[d, l, 1] - wind[l, 1] + COLS) & (COLS - 1)
            a = px * num
            qv = floor_div(a, den)
            tile = (start + floor_div(px0 * num, den).astype(I32)) >> 7
            relb[d * LAYERS + l] = start + qv.astype(I32) - tile * 128
            frac[d * LAYERS + l] = (a - qv * den) / den

    cc = iota((NPR, CHIPS * 32), 1)
    mrow, lj = cc >> 5, cc & 31
    lay = jnp.where(lj >= 20, 2, jnp.where(lj >= 10, 1, 0))
    lane_tile = lj - lay * 10
    weights = jnp.zeros((NPR, CHIPS * 32), F32)
    pupil = (b * NPR + iota((NPR, 1), 0)).astype(F32)
    for l in range(LAYERS):
        num = ratio[q, l, 0].astype(F32)
        den = ratio[q, l, 1].astype(F32)
        start = (offs[q, l, 0] - wind[l, 0] + ROWS) & (ROWS - 1)
        a = pupil * num
        qv = floor_div(a, den)
        f = (a - qv * den) / den
        base = (start + qv.astype(I32)) & 63
        high = f.astype(BF16).astype(F32)
        low = (1.0 - f).astype(BF16).astype(F32)
        w = jnp.where(mrow == base, low, 0.0) + jnp.where(mrow == ((base + 1) & 63), high, 0.0)
        weights = weights + jnp.where((lay == l) & (lane_tile < 10), w, 0.0)
    wrow[...] = weights
    for j in range(JT):
        wbig[j * NPR:(j + 1) * NPR] = jnp.where(lane_tile == j, wrow[...], 0.0).astype(BF16)

    g32 = jnp.where((iota((32, 32), 0) >> 4) == (iota((32, 32), 1) >> 4), 1.0, 0.0)
    g128 = jnp.where((iota((128, 128), 0) >> 4) == (iota((128, 128), 1) >> 4), 1.0, 0.0)
    for j in range(JT):
        av = amp[:, j * 128:(j + 1) * 128]
        energy = jnp.dot(g32, av * av, precision=HIGHEST, preferred_element_type=F32)
        energy = jnp.dot(energy, g128, precision=HIGHEST, preferred_element_type=F32)
        ampn[j] = av / jnp.sqrt(energy)

    stage[...] = jnp.zeros_like(stage)

    for h in halos:
        h.wait()
    tn = (((0,), (0,)), ((), ()))
    hr_i, hr_c = iota((8, BLK), 0), iota((8, BLK), 1)
    for l in range(LAYERS):
        w1 = wind[l, 1]
        main = jnp.where(ro == ri - w1, 1.0, 0.0).astype(BF16)
        left_m = jnp.where(hr_i - 8 == hr_c - w1, 1.0, 0.0).astype(BF16)
        right_m = jnp.where(hr_i + BLK == hr_c - w1, 1.0, 0.0).astype(BF16)
        val = jnp.dot(x[l], main, preferred_element_type=F32)
        val = val + lax.dot_general(halo_r[0, l], left_m, tn, preferred_element_type=F32)
        val = val + lax.dot_general(halo_r[1, l], right_m, tn, preferred_element_type=F32)
        y[l] = val.astype(BF16)
        edge_s[0, l] = val[BLK - 8:].astype(BF16)
        edge_s[1, l] = val[:8].astype(BF16)
    edges = [
        pltpu.make_async_remote_copy(
            src_ref=edge_s.at[i], dst_ref=edge_r.at[i], send_sem=es.at[i], recv_sem=er.at[i],
            device_id=dev, device_id_type=MESH)
        for i, dev in enumerate((up, down))
    ]
    for e in edges:
        e.start()

    def columns(l):
        def one(i, _):
            d, j = i // JT, i % JT
            num, den = ratio[d, l, 0], ratio[d, l, 1]
            start = (offs[d, l, 1] - wind[l, 1] + COLS) & (COLS - 1)
            tile = (start + stretch(j, 128, num, den, magic[den])) >> 7
            rel = relb[d * LAYERS + l, pl.ds(j, 1), :]
            f = frac[d * LAYERS + l, pl.ds(j, 1), :]
            high = f.astype(BF16).astype(F32)
            low = (1.0 - f).astype(BF16).astype(F32)
            rel = jnp.broadcast_to(rel, (8, 128))
            rel_u = rel + 1
            idx, idx_u = rel & 127, rel_u & 127
            sel, sel_u = rel >> 7, rel_u >> 7
            for h in range(2):
                t = [recv1[l][h, (tile + s) & 127].astype(F32) for s in range(3)]
                g = [jnp.take_along_axis(v, idx, axis=1) for v in t]
                u = [jnp.take_along_axis(v, idx_u, axis=1) for v in t]
                vb = jnp.where(sel == 0, g[0], jnp.where(sel == 1, g[1], g[2]))
                vu = jnp.where(sel_u == 0, u[0], jnp.where(sel_u == 1, u[1], u[2]))
                out = low * vb + high * vu
                e_buf.at[d % 2, l, d // 2, h].reshape(128, 128)[pl.ds(j, 8, stride=16), :] = out
            return 0

        lax.fori_loop(0, DIRS * JT, one, 0)

    def swap(l):
        return pltpu.make_async_remote_copy(
            src_ref=e_buf.at[1 - c, l], dst_ref=d_buf.at[l], send_sem=ws.at[l], recv_sem=wr.at[l],
            device_id=(b, xl * 2 + 1 - c), device_id_type=MESH)

    for l in range(LAYERS):
        pltpu.make_async_copy(recv1[l], recv1[l], r1.at[l]).wait()
        columns(l)
        swap(l).start()
        if l == 0:
            for e in edges:
                e.wait()
            for k in range(LAYERS):
                w0 = wind[k, 0]
                main = jnp.where(ri == ro - w0, 1.0, 0.0).astype(BF16)
                er_r, er_i = iota((BLK, 8), 0), iota((BLK, 8), 1)
                top_m = jnp.where(er_i - 8 == er_r - w0, 1.0, 0.0).astype(BF16)
                bot_m = jnp.where(er_i + BLK == er_r - w0, 1.0, 0.0).astype(BF16)
                val = jnp.dot(main, y[k], preferred_element_type=F32)
                val = val + jnp.dot(top_m, edge_r[0, k], preferred_element_type=F32)
                val = val + jnp.dot(bot_m, edge_r[1, k], preferred_element_type=F32)
                x[k] = val.astype(BF16)
                pltpu.make_async_copy(x.at[k], new_out.at[k], osem.at[k]).start()

    for l in range(LAYERS):
        swap(l).wait()

    def send_rows(p, _):
        for pxl in range(2):
            for l in range(LAYERS):
                num, den = ratio[pxl * 2 + c, l, 0], ratio[pxl * 2 + c, l, 1]
                s = (offs[pxl * 2 + c, l, 0] - wind[l, 0] + ROWS + stretch(p, NPR, num, den, magic[den])) & (ROWS - 1)
                row = (s + ((chip - s) & 63)) & (ROWS - 1)
                k = row >> 6
                h, cs, kk = k >> 4, (k >> 3) & 1, k & 7
                mine = e_buf[c, l, pxl, h, kk]
                other = d_buf[l, pxl, h, kk]
                keep = jnp.where(cs == c, 1, 0)
                val = jnp.where(jnp.broadcast_to(keep, (16, 128)) == 1, mine, other)
                stage[pxl, l * 10:l * 10 + 10, :] = val[:10]
            send2[p * 2 + pxl] = stage[pxl].astype(BF16)
        return 0

    lax.fori_loop(0, 32, send_rows, 0)

    def go2(k, _):
        pb, pxl = shift_at((b, xl), k)
        pltpu.make_async_remote_copy(
            src_ref=send2.at[pb * 2 + pxl], dst_ref=recv2.at[chip],
            send_sem=s2, recv_sem=r2,
            device_id=device(pb, pxl), device_id_type=MESH,
        ).start()
        return 0

    lax.fori_loop(1, CHIPS, go2, 0)
    pltpu.make_async_copy(send2.at[chip], recv2.at[chip], r2).start()
    pltpu.make_async_copy(recv2, recv2, r2).wait()

    phase = jnp.dot(wbig[...], recv2[...].reshape(CHIPS * 32, 128), preferred_element_type=F32)
    for j in range(JT):
        sin, cos = sincos(phase[j * NPR:(j + 1) * NPR])
        field[0, j] = ampn[j] * cos
        field[1, j] = ampn[j] * sin
    for j in range(JT):
        both = jnp.concatenate([field[0, j], field[1, j]], axis=0)
        g = jnp.dot(both, dcol[...], precision=HIGHEST, preferred_element_type=F32)
        half_re = g[:32, :256] - g[32:, 256:]
        half_im = g[:32, 256:] + g[32:, :256]
        half = jnp.concatenate([half_re, half_im], axis=0)
        full = jnp.dot(drow[...], half, precision=HIGHEST, preferred_element_type=F32)
        spots[:, j * 256:(j + 1) * 256] = full[:64] * full[:64] + full[64:] * full[64:]

    for l in range(LAYERS):
        pltpu.make_async_copy(send1.at[l, 0:63], send1.at[l, 0:63], s1.at[l]).wait()
        pltpu.make_async_copy(x.at[l], new_out.at[l], osem.at[l]).wait()
    pltpu.make_async_copy(send2.at[0:63], send2.at[0:63], s2).wait()


def group(b, xl, k, axis):
    xh, y, z = b // 16, (b // 4) % 4, b % 4
    if axis == 0:
        pos = (xl * 4 + z + k) % 8
        return xh * 16 + y * 4 + pos % 4, pos // 4
    pos = (xh * 4 + y + k) % 8
    return (pos // 4) * 16 + (pos % 4) * 4 + z, xl


def per_device(screens, amplitude, wind, offsets, ratio):
    cols, rows = dft_tables()
    vmem = pl.BlockSpec(memory_space=pltpu.VMEM)
    smem = pl.BlockSpec(memory_space=pltpu.SMEM)
    hbm = pl.BlockSpec(memory_space=pl.ANY)
    dma, reg = pltpu.SemaphoreType.DMA, pltpu.SemaphoreType.REGULAR
    new, spots = pl.pallas_call(
        kernel,
        out_shape=(
            jax.ShapeDtypeStruct((LAYERS, BLK, BLK), BF16),
            jax.ShapeDtypeStruct((64, 2560), F32),
        ),
        in_specs=[smem, smem, smem, smem, hbm, vmem, vmem, vmem],
        out_specs=(hbm, vmem),
        scratch_shapes=[
            pltpu.VMEM((LAYERS, BLK, BLK), BF16),
            pltpu.VMEM((LAYERS, CHIPS, 4, 8, 128), BF16),
            pltpu.VMEM((2, 128, 8, 128), BF16),
            pltpu.VMEM((2, 128, 8, 128), BF16),
            pltpu.VMEM((2, 128, 8, 128), BF16),
            pltpu.VMEM((2, LAYERS, 8, BLK), BF16),
            pltpu.VMEM((2, LAYERS, 8, BLK), BF16),
            pltpu.VMEM((2, LAYERS, 8, BLK), BF16),
            pltpu.VMEM((2, LAYERS, 8, BLK), BF16),
            pltpu.VMEM((LAYERS, BLK, BLK), BF16),
            pltpu.VMEM((DIRS * LAYERS, 16, 128), I32),
            pltpu.VMEM((DIRS * LAYERS, 16, 128), F32),
            pltpu.VMEM((LAYERS, 2, 2, 8, 16, 128), F32),
            pltpu.VMEM((2, LAYERS, 2, 2, 8, 16, 128), F32),
            pltpu.VMEM((2, 32, 128), F32),
            pltpu.VMEM((CHIPS, 32, 128), BF16),
            pltpu.VMEM((CHIPS, 32, 128), BF16),
            pltpu.VMEM((NPR, CHIPS * 32), F32),
            pltpu.VMEM((JT * NPR, CHIPS * 32), BF16),
            pltpu.VMEM((JT, NPR, 128), F32),
            pltpu.VMEM((2, JT, NPR, 128), F32),
            dma((3,)), dma((3,)), dma((3,)), dma((2,)), dma((2,)), dma((2,)), dma((2,)),
            dma((3,)), dma((3,)), dma, dma, dma((3,)), reg,
        ],
        compiler_params=pltpu.CompilerParams(
            collective_id=0, has_side_effects=True, vmem_limit_bytes=48 << 20),
        name="screens_to_spots",
    )(wind, offsets, ratio, jnp.asarray(reciprocals()), screens, amplitude, jnp.asarray(cols), jnp.asarray(rows))
    return new, spots[None]


def solution(mesh):
    return jax.shard_map(
        per_device,
        mesh=mesh,
        in_specs=(P(None, "dir", "layer"), P("layer", None), P(), P(), P()),
        out_specs=(P(None, "dir", "layer"), P("dir", "layer", None)),
        check_vma=False,
    )
```

time: 354 us -> 78.3 us (0.22)
  waiting for transfers between devices: 236 us -> 0 us
  Pallas kernels: 0 us -> 67.8 us
  matrix products: 43.4 us -> 0 us
  between operations: 29.6 us -> 0.64 us
  other arithmetic: 23.6 us -> 0 us
  starting transfers between devices: 11.2 us -> 0 us
    reduce_scatter x1 -> x0, waiting for transfers between devices: 191 us -> none  [per_device(): lax.psum_scatter(total.astype(jnp.bfloat16), 'layer', scatter_dimension=0...]
    pallas_call x0 -> x1, Pallas kernels: none -> 67.8 us  [per_device(): pl.pallas_call(kernel, out_shape=(jax.ShapeDtypeStruct((LAYERS, BLK, BLK)...]
    dot_general x11 -> x0, matrix products: 43.4 us -> none  [the longest x3 25.4 us: per_device(): jnp.dot(projected[level], col_weights[level], preferred_element_type=jnp....]
    all_gather x1 -> x0, waiting for transfers between devices: 36.3 us -> none  [per_device(): piece = lax.all_gather(new_screens, 'dir', axis=1, tiled=True)]
    select_n x6 -> x0, other arithmetic: 12.1 us -> none  [spans(): upper = (base + 1) % length]
    ppermute x4 -> x0, starting transfers between devices: 11 us -> none  [the longest x2 8.84 us: with_halo(): after = lax.ppermute(initial, axis, down)]
    unnamed x10 -> x15, local copies, waits for them, and re-layouts: 0.02 us -> 9.11 us
    ppermute x4 -> x0, waiting for transfers between devices: 9.04 us -> none  [the longest x2 9.03 us: with_halo(): before = lax.ppermute(last, axis, up)]
  transfers between devices with their start and end apart: 6 -> 0, of which waited for: 3 -> 0; matrix products, arithmetic and copies ran while one was open for 6% -> 0% of each run, Pallas kernels for 0% -> 0%
where the time goes in v1:
time: 78.3 us; the launch traced here: 77.5 us
  Pallas kernels  67.8 us (87%)
  local copies, waits for them, and re-layouts  9.11 us (12%)
    pallas_call x1, Pallas kernels, per_device(): pl.pallas_call(kernel, out_shape=(jax.ShapeDtypeStruct((LAYERS, BLK, BLK)...  67.8 us
    unnamed x15, local copies, waits for them, and re-layouts  9.11 us

profile of v1, /device:TPU:0, one launch (start us, length us, event | category | flops | bytes accessed | tf_op | source)
XLA Modules:
  0.0 77.5 jit_solution(16290292986690640465)
XLA Ops:
  0.6 0.8 copy.10.wind
  1.4 0.8 %copy.11.offs = s32[4,3,2]{2,1,0:T(4,128)S(1)} copy(s32[4,3,2]{0,2,1:T(2,128)} %param.11) | data formatting | bytes 192 | tf_op args[3]
  2.2 0.8 %copy.12.ratio = s32[4,3,2]{2,1,0:T(4,128)S(1)} copy(s32[4,3,2]{0,2,1:T(2,128)} %param.12) | data formatting | bytes 192 | tf_op args[4]
  3.0 0.0 copy-start
  3.0 1.4 %copy-done = bf16[3,512,512]{2,1,0:T(8,128)(2,1)S(1)} copy-done((bf16[3,512,512]{2,1,0:T(8,128)(2,1)S(1)}, bf16[3,512,512]{2,1,0:T(8,128)(2,1)}, u32[]{:S(2)}) %copy-start) | copy-done | bytes 1572888
  4.4 0.0 copy-start.1
  4.4 0.9 %copy-done.1 = f32[128,512]{1,0:T(8,128)S(1)} copy-done((f32[128,512]{1,0:T(8,128)S(1)}, f32[128,512]{1,0:T(8,128)}, u32[]{:S(2)}) %copy-start.1) | copy-done | bytes 262168
  5.3 0.0 copy-start.2
  5.3 0.9 %copy-done.2 = f32[32,1280]{1,0:T(8,128)S(1)} copy-done((f32[32,1280]{1,0:T(8,128)S(1)}, f32[32,1280]{1,0:T(8,128)}, u32[]{:S(2)}) %copy-start.2) | copy-done | bytes 163864
  6.2 0.0 copy-start.3
  6.2 0.8 %copy-done.3 = f32[128,64]{1,0:T(8,128)S(1)} copy-done((f32[128,64]{1,0:T(8,128)S(1)}, f32[128,64]{1,0:T(8,128)}, u32[]{:S(2)}) %copy-start.3) | copy-done | bytes 32792
  7.1 0.0 copy-start.4
  7.1 0.7 copy-done.4
  7.8 67.8 %screens_to_spots.1 = (bf16[3,512,512]{2,1,0:T(8,128)(2,1)S(1)}, f32[64,2560]{1,0:T(8,128)S(1)}) custom-call(s32[3,2]{1,0:T(4,128)S(1)} %copy.10.wind, s32[4,3,2]{2,1,0:T(4,128)S(1)} %copy.11.offs, s32[4,3,2]{2,1,0:T(4,128)S(1)} %copy.12.ratio, s32[129]{0:T(256)S(1)} %copy-done.4, bf16[3,512,512]{2,1,0:T(8,128)(2,1)S(1)} %copy-done, ...), custom_call_target="tpu_custom_call" | custom-call | tf_op jit(solution)/shard_map/screens_to_spots/pallas_call | solution.py:376
  75.5 1.1 %copy.15 = bf16[3,512,512]{2,1,0:T(8,128)(2,1)} copy(bf16[3,512,512]{2,1,0:T(8,128)(2,1)S(1)} %get-tuple-element.8) | data formatting | bytes 3145728
  76.7 0.8 %copy.16 = f32[1,64,2560]{2,1,0:T(8,128)} copy(f32[1,64,2560]{2,1,0:T(8,128)S(1)} %bitcast.1) | data formatting | bytes 1310720
Async XLA Ops:
  3.0 1.4 %copy-start = (bf16[3,512,512]{2,1,0:T(8,128)(2,1)S(1)}, bf16[3,512,512]{2,1,0:T(8,128)(2,1)}, u32[]{:S(2)}) copy-start(bf16[3,512,512]{2,1,0:T(8,128)(2,1)} %screens.1) | copy-start | bytes 4718596
  4.4 0.9 %copy-start.1 = (f32[128,512]{1,0:T(8,128)S(1)}, f32[128,512]{1,0:T(8,128)}, u32[]{:S(2)}) copy-start(f32[128,512]{1,0:T(8,128)} %constant.7.clone.dcol) | copy-start | bytes 786436
  5.3 0.9 %copy-start.2 = (f32[32,1280]{1,0:T(8,128)S(1)}, f32[32,1280]{1,0:T(8,128)}, u32[]{:S(2)}) copy-start(f32[32,1280]{1,0:T(8,128)} %amp.1) | copy-start | bytes 491524
  6.2 0.8 %copy-start.3 = (f32[128,64]{1,0:T(8,128)S(1)}, f32[128,64]{1,0:T(8,128)}, u32[]{:S(2)}) copy-start(f32[128,64]{1,0:T(8,128)} %constant.8.clone.drow) | copy-start | bytes 98308
  7.1 0.7 copy-start.4

commit v2 on v1

v2 whole, which is shorter than its diff:
```python
import jax
import jax.numpy as jnp
import numpy as np
from jax import lax
from jax.experimental import pallas as pl
from jax.experimental.pallas import tpu as pltpu
from jax.sharding import PartitionSpec as P

MESH = pl.DeviceIdType.MESH
SUB = 16
SPOT = 32
HALO = 8
LAYERS = 3
DIRS = 4
ROWS, COLS = 2048, 16384
PR, PC = 1024, 1280
BLK = 512
CHIPS = 64
JT = PC // 128
NPR = 32
F32, BF16, I32 = jnp.float32, jnp.bfloat16, jnp.int32
HIGHEST = lax.Precision.HIGHEST


def iota(shape, dim):
    return lax.broadcasted_iota(I32, shape, dim)


def floor_div(a, den):
    q = jnp.floor(a / den)
    r = a - q * den
    q = q + jnp.where(r >= den, 1.0, 0.0) - jnp.where(r < 0.0, 1.0, 0.0)
    return q


def reciprocals():
    den = np.maximum(np.arange(129), 1)
    return (2 ** 21 // den + 1).astype(np.int32)


def stretch(i, unit, num, den, mul):
    part = i * (num - den)
    whole = (part * mul) >> 21
    rest = part - whole * den
    return unit * (i + whole) + ((unit * rest * mul) >> 21)


def sincos(x):
    n = jnp.floor(x * np.float32(2.0 / np.pi) + 0.5)
    r = x - n * np.float32(1.5703125)
    r = r - n * np.float32(4.837512969970703125e-4)
    r = r - n * np.float32(7.54978995489188216e-8)
    r2 = r * r
    s = r + r * r2 * (
        np.float32(-1.6666654611e-1)
        + r2 * (np.float32(8.3321608736e-3) + r2 * np.float32(-1.9515295891e-4))
    )
    c = (
        1.0
        - 0.5 * r2
        + r2 * r2 * (
            np.float32(4.166664568298827e-2)
            + r2 * (np.float32(-1.388731625493765e-3) + r2 * np.float32(2.443315711809948e-5))
        )
    )
    k = n.astype(I32)
    swap = (k & 1) == 1
    sin = jnp.where(swap, c, s)
    cos = jnp.where(swap, s, c)
    sin = jnp.where((k & 2) == 2, -sin, sin)
    cos = jnp.where(((k + 1) & 2) == 2, -cos, cos)
    return sin, cos


def dft_tables():
    turns = ((np.arange(SPOT)[:, None] - SPOT // 2) * np.arange(SUB)[None, :]) % SPOT
    angle = turns * (2.0 * np.pi / SPOT)
    c, s = np.cos(angle), -np.sin(angle)
    cols = np.concatenate([np.kron(np.eye(8), c.T), np.kron(np.eye(8), s.T)], axis=1)
    cb, sb = np.kron(np.eye(2), c), np.kron(np.eye(2), s)
    rows = np.block([[cb, -sb], [sb, cb]])
    return cols.astype(np.float32), rows.astype(np.float32)


def shift_at(b, xl, k):
    px = ((b >> 4) * 2 + xl + (k & 3)) & 3
    py = ((b >> 2) + (k >> 2)) & 3
    pz = (b + (k >> 4)) & 3
    return (px >> 1) * 16 + py * 4 + pz, px & 1


def kernel(
    wind, offs, ratio, magic, screens, amp_h, dcol_h, drow_h,
    new_out, spots,
    x, amp, dcol, drow, send1, recv_a, recv_b, recv_c, halo_s, halo_r, edge_s, edge_r, y,
    relb, frac, b_a, b_b, b_c, send2a, send2b, recv2a, recv2b, wbig_a, wbig_b, ampn, phase, field,
    in_sem, tab_sem, s1, r1, hs, hr, es, er, ws, wr, s2, r2, osem,
):
    recv1, cols = (recv_a, recv_b, recv_c), (b_a, b_b, b_c)
    b = lax.axis_index("layer")
    q = lax.axis_index("dir")
    xl, c = q // 2, q % 2
    chip = b * 2 + xl

    def device(pb, pxl):
        return (pb, pxl * 2 + c)

    up = (b, (q + 1) % 4)
    down = (b, (q + 3) % 4)
    right = ((b + 1) % 32, q)
    left = ((b + 31) % 32, q)
    bar = pltpu.get_barrier_semaphore()
    for dev in (up, down):
        pl.semaphore_signal(bar, inc=1, device_id=dev, device_id_type=MESH)

    def greet(k, _):
        pl.semaphore_signal(bar, inc=1, device_id=device(*shift_at(b, xl, 64 - k)), device_id_type=MESH)
        return 0

    lax.fori_loop(1, CHIPS, greet, 0)

    loads = [pltpu.make_async_copy(screens.at[l], x.at[l], in_sem.at[l]) for l in range(LAYERS)]
    tables = [
        pltpu.make_async_copy(src, dst, tab_sem.at[i])
        for i, (src, dst) in enumerate(((amp_h, amp), (dcol_h, dcol), (drow_h, drow)))
    ]
    for load in loads + tables:
        load.start()

    ro, ri = iota((BLK, BLK), 0), iota((BLK, BLK), 1)
    perm = jnp.where(ri == (ro & 7) * 64 + (ro >> 3), 1.0, 0.0).astype(BF16)

    def permute(l):
        loads[l].wait()
        rows = jnp.dot(perm, x[l], preferred_element_type=F32)
        for t in range(4):
            send1[l, :, t] = rows[:, t * 128:(t + 1) * 128].reshape(CHIPS, 8, 128).astype(BF16)

    def exchange(l):
        def go(k, _):
            pb, pxl = shift_at(b, xl, 64 - k)
            pltpu.make_async_remote_copy(
                src_ref=send1.at[l, pb * 2 + pxl],
                dst_ref=recv1[l].at[xl, pl.ds(b * 4, 4)],
                send_sem=s1.at[l], recv_sem=r1.at[l],
                device_id=device(pb, pxl), device_id_type=MESH,
            ).start()
            return 0

        lax.fori_loop(1, CHIPS, go, 0)
        pltpu.make_async_copy(send1.at[l, chip], recv1[l].at[xl, pl.ds(b * 4, 4)], r1.at[l]).start()

    permute(0)
    pl.semaphore_wait(bar, 65)
    exchange(0)
    permute(1)
    exchange(1)
    permute(2)
    exchange(2)

    lane8, row8 = iota((8, 128), 1), iota((8, 128), 0)
    first = jnp.where(lane8 == row8, 1.0, 0.0).astype(BF16)
    last = jnp.where(lane8 == row8 + 120, 1.0, 0.0).astype(BF16)
    nt = (((1,), (1,)), ((), ()))
    for l in range(LAYERS):
        halo_s[0, l] = lax.dot_general(
            last, x[l, :, BLK - 128:], nt, preferred_element_type=F32).astype(BF16)
        halo_s[1, l] = lax.dot_general(
            first, x[l, :, :128], nt, preferred_element_type=F32).astype(BF16)
    halos = [
        pltpu.make_async_remote_copy(
            src_ref=halo_s.at[i], dst_ref=halo_r.at[i], send_sem=hs.at[i], recv_sem=hr.at[i],
            device_id=dev, device_id_type=MESH)
        for i, dev in enumerate((right, left))
    ]
    for h in halos:
        h.start()

    px0 = (iota((16, 128), 0) * 128).astype(F32)
    px = px0 + iota((16, 128), 1).astype(F32)
    for d in range(DIRS):
        for l in range(LAYERS):
            num = ratio[l, 0, d].astype(F32)
            den = ratio[l, 1, d].astype(F32)
            start = (offs[l, 1, d] - wind[1, l] + COLS) & (COLS - 1)
            a = px * num
            qv = floor_div(a, den)
            tile = (start + floor_div(px0 * num, den).astype(I32)) >> 7
            relb[d * LAYERS + l] = start + qv.astype(I32) - tile * 128
            frac[d * LAYERS + l] = (a - qv * den) / den

    pupil = (b * NPR + iota((NPR, 1), 0)).astype(F32)

    def row_weights(l, mrow):
        num = ratio[l, 0, q].astype(F32)
        den = ratio[l, 1, q].astype(F32)
        start = (offs[l, 0, q] - wind[0, l] + ROWS) & (ROWS - 1)
        a = pupil * num
        qv = floor_div(a, den)
        f = (a - qv * den) / den
        base = (start + qv.astype(I32)) & 63
        high = f.astype(BF16).astype(F32)
        low = (1.0 - f).astype(BF16).astype(F32)
        return jnp.where(mrow == base, low, 0.0) + jnp.where(mrow == ((base + 1) & 63), high, 0.0)

    ca = iota((NPR, CHIPS * 24), 1)
    ma = (ca * 2731) >> 16
    ja = ca - ma * 24
    wa = jnp.where(ja < 10, row_weights(0, ma), row_weights(1, ma))
    for j in range(JT):
        wbig_a[j * NPR:(j + 1) * NPR] = jnp.where((ja == j) | (ja == j + 10), wa, 0.0).astype(BF16)
    cb = iota((NPR, CHIPS * 16), 1)
    wb = row_weights(2, cb >> 4)
    for j in range(JT):
        wbig_b[j * NPR:(j + 1) * NPR] = jnp.where((cb & 15) == j, wb, 0.0).astype(BF16)

    for load in tables:
        load.wait()
    g32 = jnp.where((iota((32, 32), 0) >> 4) == (iota((32, 32), 1) >> 4), 1.0, 0.0)
    g128 = jnp.where((iota((128, 128), 0) >> 4) == (iota((128, 128), 1) >> 4), 1.0, 0.0)
    for j in range(JT):
        av = amp[:, j * 128:(j + 1) * 128]
        energy = jnp.dot(g32, av * av, precision=HIGHEST, preferred_element_type=F32)
        energy = jnp.dot(energy, g128, precision=HIGHEST, preferred_element_type=F32)
        ampn[j] = av / jnp.sqrt(energy)

    for h in halos:
        h.wait()
    tn = (((0,), (0,)), ((), ()))
    lane = iota((BLK, 128), 1)
    for l in range(LAYERS):
        w1 = wind[1, l]
        lanes = [lax.dot_general(halo_r[0, l], last, tn, preferred_element_type=F32)]
        lanes += [x[l, :, t * 128:(t + 1) * 128].astype(F32) for t in range(4)]
        lanes += [lax.dot_general(halo_r[1, l], first, tn, preferred_element_type=F32)]
        turned = [pltpu.roll(v, (w1 + 128) & 127, 1) for v in lanes]
        before, after = lane < w1, lane >= 128 + w1
        for t in range(4):
            val = jnp.where(before, turned[t], jnp.where(after, turned[t + 2], turned[t + 1]))
            y[l, 8:8 + BLK, t * 128:(t + 1) * 128] = val
        edge_s[0, l] = y[l, BLK:BLK + 8].astype(BF16)
        edge_s[1, l] = y[l, 8:16].astype(BF16)
    edges = [
        pltpu.make_async_remote_copy(
            src_ref=edge_s.at[i], dst_ref=edge_r.at[i], send_sem=es.at[i], recv_sem=er.at[i],
            device_id=dev, device_id_type=MESH)
        for i, dev in enumerate((up, down))
    ]
    for e in edges:
        e.start()

    def flow_rows():
        for e in edges:
            e.wait()
        for l in range(LAYERS):
            y[l, 0:8] = edge_r[0, l].astype(F32)
            y[l, BLK + 8:BLK + 16] = edge_r[1, l].astype(F32)
            w0 = wind[0, l]
            turn, whole = w0 & 7, w0 >> 3
            keep = iota((BLK // 8 + 1, 8, 128), 1) >= turn
            for t in range(4):
                part = y[l, :, t * 128:(t + 1) * 128].reshape(BLK // 8 + 2, 8, 128)
                part = pltpu.roll(part, turn, 1)
                part = jnp.concatenate([part[:1], jnp.where(keep, part[1:], part[:-1])], axis=0)
                val = jnp.where(whole > 0, part[:-2], jnp.where(whole == 0, part[1:-1], part[2:]))
                x[l, :, t * 128:(t + 1) * 128] = val.reshape(BLK, 128).astype(BF16)
            pltpu.make_async_copy(x.at[l], new_out.at[l], osem.at[l]).start()

    def columns(l):
        def one(i, _):
            d, j = i // JT, i % JT
            num, den = ratio[l, 0, d], ratio[l, 1, d]
            start = (offs[l, 1, d] - wind[1, l] + COLS) & (COLS - 1)
            tile = (start + stretch(j, 128, num, den, magic[den])) >> 7
            rel = relb[d * LAYERS + l, pl.ds(j, 1), :]
            f = frac[d * LAYERS + l, pl.ds(j, 1), :]
            high = f.astype(BF16).astype(F32)
            low = (1.0 - f).astype(BF16).astype(F32)
            rel = jnp.broadcast_to(rel, (8, 128))
            rel_u = rel + 1
            idx, idx_u = rel & 127, rel_u & 127
            sel, sel_u = rel >> 7, rel_u >> 7
            for h in range(2):
                t = [recv1[l][h, (tile + s) & 127].astype(F32) for s in range(3)]
                g = [jnp.take_along_axis(v, idx, axis=1) for v in t]
                u = [jnp.take_along_axis(v, idx_u, axis=1) for v in t]
                vb = jnp.where(sel == 0, g[0], jnp.where(sel == 1, g[1], g[2]))
                vu = jnp.where(sel_u == 0, u[0], jnp.where(sel_u == 1, u[1], u[2]))
                out = low * vb + high * vu
                cols[l].at[d % 2, c, d // 2, h].reshape(128, 128)[pl.ds(j, 8, stride=16), :] = out
            return 0

        lax.fori_loop(0, DIRS * JT, one, 0)

    def swap(l):
        return pltpu.make_async_remote_copy(
            src_ref=cols[l].at[1 - c, c], dst_ref=cols[l].at[1 - c, c],
            send_sem=ws.at[l], recv_sem=wr.at[l],
            device_id=(b, xl * 2 + 1 - c), device_id_type=MESH)

    def arrive(l):
        pltpu.make_async_copy(recv1[l], recv1[l], r1.at[l]).wait()
        columns(l)
        swap(l).start()

    def row_of(l, p, pxl):
        d = pxl * 2 + c
        num, den = ratio[l, 0, d], ratio[l, 1, d]
        s = offs[l, 0, d] - wind[0, l] + ROWS + stretch(p, NPR, num, den, magic[den])
        k = ((s + ((chip - s) & 63)) & (ROWS - 1)) >> 6
        val = cols[l][c, (k >> 3) & 1, pxl, k >> 4, k & 7]
        return val[:8], val[8:]

    sub = iota((8, 128), 0)

    def deliver(src, dst, i, k, pb, pxl):
        @pl.when(k > 0)
        def _():
            pltpu.make_async_remote_copy(
                src_ref=src.at[pb * 2 + pxl], dst_ref=dst.at[chip],
                send_sem=s2.at[i], recv_sem=r2.at[i],
                device_id=device(pb, pxl), device_id_type=MESH,
            ).start()

        @pl.when(k == 0)
        def _():
            pltpu.make_async_copy(src.at[chip], dst.at[chip], r2.at[i]).start()

    def send_a(i, _):
        k = 63 - i
        pb, pxl = shift_at(b, xl, k)
        a0, a1 = row_of(0, pb, pxl)
        b0, b1 = row_of(1, pb, pxl)
        b0, b1 = pltpu.roll(b0, 2, 0), pltpu.roll(b1, 2, 0)
        send2a[pb * 2 + pxl, 0] = a0.astype(BF16)
        send2a[pb * 2 + pxl, 1] = jnp.where(sub < 2, a1, b0).astype(BF16)
        send2a[pb * 2 + pxl, 2] = jnp.where(sub < 2, b0, jnp.where(sub < 4, b1, 0.0)).astype(BF16)
        deliver(send2a, recv2a, 0, k, pb, pxl)
        return 0

    def send_b(i, _):
        k = 63 - i
        pb, pxl = shift_at(b, xl, k)
        a0, a1 = row_of(2, pb, pxl)
        send2b[pb * 2 + pxl, 0] = a0.astype(BF16)
        send2b[pb * 2 + pxl, 1] = jnp.where(sub < 2, a1, 0.0).astype(BF16)
        deliver(send2b, recv2b, 1, k, pb, pxl)
        return 0

    arrive(0)
    flow_rows()
    arrive(1)
    swap(0).wait()
    swap(1).wait()
    lax.fori_loop(0, CHIPS, send_a, 0)
    arrive(2)
    swap(2).wait()
    lax.fori_loop(0, CHIPS, send_b, 0)

    pltpu.make_async_copy(recv2a, recv2a, r2.at[0]).wait()
    phase[...] = jnp.dot(
        wbig_a[...], recv2a[...].reshape(CHIPS * 24, 128), preferred_element_type=F32)
    pltpu.make_async_copy(recv2b, recv2b, r2.at[1]).wait()
    phase[...] += jnp.dot(
        wbig_b[...], recv2b[...].reshape(CHIPS * 16, 128), preferred_element_type=F32)
    for j in range(JT):
        sin, cos = sincos(phase[j * NPR:(j + 1) * NPR])
        field[0, j] = ampn[j] * cos
        field[1, j] = ampn[j] * sin
    for j in range(JT):
        both = jnp.concatenate([field[0, j], field[1, j]], axis=0)
        g = jnp.dot(both, dcol[...], precision=HIGHEST, preferred_element_type=F32)
        half_re = g[:32, :256] - g[32:, 256:]
        half_im = g[:32, 256:] + g[32:, :256]
        half = jnp.concatenate([half_re, half_im], axis=0)
        full = jnp.dot(drow[...], half, precision=HIGHEST, preferred_element_type=F32)
        spots[:, j * 256:(j + 1) * 256] = full[:64] * full[:64] + full[64:] * full[64:]

    for l in range(LAYERS):
        pltpu.make_async_copy(send1.at[l, 0:63], send1.at[l, 0:63], s1.at[l]).wait()
        pltpu.make_async_copy(x.at[l], new_out.at[l], osem.at[l]).wait()
    pltpu.make_async_copy(send2a.at[0:63], send2a.at[0:63], s2.at[0]).wait()
    pltpu.make_async_copy(send2b.at[0:63], send2b.at[0:63], s2.at[1]).wait()


def per_device(screens, amplitude, wind, offsets, ratio):
    cols, rows = dft_tables()
    vmem = pl.BlockSpec(memory_space=pltpu.VMEM)
    smem = pl.BlockSpec(memory_space=pltpu.SMEM)
    hbm = pl.BlockSpec(memory_space=pl.ANY)
    dma = pltpu.SemaphoreType.DMA
    new, spots = pl.pallas_call(
        kernel,
        out_shape=(
            jax.ShapeDtypeStruct((LAYERS, BLK, BLK), BF16),
            jax.ShapeDtypeStruct((64, 2560), F32),
        ),
        in_specs=[smem, smem, smem, smem, hbm, hbm, hbm, hbm],
        out_specs=(hbm, vmem),
        scratch_shapes=[
            pltpu.VMEM((LAYERS, BLK, BLK), BF16),
            pltpu.VMEM((NPR, PC), F32),
            pltpu.VMEM((128, 512), F32),
            pltpu.VMEM((128, 64), F32),
            pltpu.VMEM((LAYERS, CHIPS, 4, 8, 128), BF16),
            pltpu.VMEM((2, 128, 8, 128), BF16),
            pltpu.VMEM((2, 128, 8, 128), BF16),
            pltpu.VMEM((2, 128, 8, 128), BF16),
            pltpu.VMEM((2, LAYERS, 8, BLK), BF16),
            pltpu.VMEM((2, LAYERS, 8, BLK), BF16),
            pltpu.VMEM((2, LAYERS, 8, BLK), BF16),
            pltpu.VMEM((2, LAYERS, 8, BLK), BF16),
            pltpu.VMEM((LAYERS, BLK + 16, BLK), F32),
            pltpu.VMEM((DIRS * LAYERS, 16, 128), I32),
            pltpu.VMEM((DIRS * LAYERS, 16, 128), F32),
            pltpu.VMEM((2, 2, 2, 2, 8, 16, 128), F32),
            pltpu.VMEM((2, 2, 2, 2, 8, 16, 128), F32),
            pltpu.VMEM((2, 2, 2, 2, 8, 16, 128), F32),
            pltpu.VMEM((CHIPS, 3, 8, 128), BF16),
            pltpu.VMEM((CHIPS, 2, 8, 128), BF16),
            pltpu.VMEM((CHIPS, 3, 8, 128), BF16),
            pltpu.VMEM((CHIPS, 2, 8, 128), BF16),
            pltpu.VMEM((JT * NPR, CHIPS * 24), BF16),
            pltpu.VMEM((JT * NPR, CHIPS * 16), BF16),
            pltpu.VMEM((JT, NPR, 128), F32),
            pltpu.VMEM((JT * NPR, 128), F32),
            pltpu.VMEM((2, JT, NPR, 128), F32),
            dma((3,)), dma((3,)), dma((3,)), dma((3,)), dma((2,)), dma((2,)), dma((2,)), dma((2,)),
            dma((3,)), dma((3,)), dma((2,)), dma((2,)), dma((3,)),
        ],
        compiler_params=pltpu.CompilerParams(
            collective_id=0, has_side_effects=True, vmem_limit_bytes=63 << 20),
        name="screens_to_spots",
    )(wind.T, offsets.transpose(1, 2, 0), ratio.transpose(1, 2, 0), jnp.asarray(reciprocals()), screens, amplitude, jnp.asarray(cols), jnp.asarray(rows))
    return new, spots[None]


def solution(mesh):
    return jax.shard_map(
        per_device,
        mesh=mesh,
        in_specs=(P(None, "dir", "layer"), P("layer", None), P(), P(), P()),
        out_specs=(P(None, "dir", "layer"), P("dir", "layer", None)),
        check_vma=False,
    )
```

time: 78.3 us -> 70.4 us (0.90)
  local copies, waits for them, and re-layouts: 9.11 us -> 3.56 us
  Pallas kernels: 67.8 us -> 65.9 us
    unnamed x15 -> x4, local copies, waits for them, and re-layouts: 9.11 us -> 3.56 us
    pallas_call x1, Pallas kernels: 67.8 us -> 65.9 us  [per_device(): pl.pallas_call(kernel, out_shape=(jax.ShapeDtypeStruct((LAYERS, BLK, BLK)...]
where the time goes in v2:
time: 70.4 us; the launch traced here: 70.1 us
  Pallas kernels  65.9 us (94%)
  local copies, waits for them, and re-layouts  3.56 us (5%)
    pallas_call x1, Pallas kernels, per_device(): pl.pallas_call(kernel, out_shape=(jax.ShapeDtypeStruct((LAYERS, BLK, BLK)...  65.9 us
    unnamed x4, local copies, waits for them, and re-layouts  3.56 us

profile of v2, /device:TPU:0, one launch (start us, length us, event | category | flops | bytes accessed | tf_op | source)
XLA Modules:
  0.0 70.1 jit_solution(5921156962755546682)
XLA Ops:
  0.6 65.9 %screens_to_spots.1 = (bf16[3,512,512]{2,1,0:T(8,128)(2,1)}, f32[64,2560]{1,0:T(8,128)}) custom-call(s32[2,3]{1,0:T(2,128)} %bitcast.7, s32[3,2,4]{2,1,0:T(2,128)} %bitcast.5, s32[3,2,4]{2,1,0:T(2,128)} %bitcast.6, s32[129]{0:T(256)} %constant.6.clone.magic, bf16[3,512,512]{2,1,0:T(8,128)(2,1)} %screens.1, f32[32,1280]{1,0:T(8,128)} %amp_h.1, ...), custom_call_target="tpu_custom_call" | custom-call | tf_op jit(solution)/shard_map/screens_to_spots/pallas_call | solution.py:392
  66.6 0.0 copy-start
  66.6 2.7 %copy.12 = bf16[3,512,512]{2,1,0:T(8,128)(2,1)} copy(bf16[3,512,512]{2,1,0:T(8,128)(2,1)} %get-tuple-element.8) | data formatting | bytes 3145728
  69.3 0.0 copy-done
  69.3 0.8 %copy.13 = f32[1,64,2560]{2,1,0:T(8,128)} copy(f32[1,64,2560]{2,1,0:T(8,128)S(1)} %bitcast.4) | data formatting | bytes 1310720
Async XLA Ops:
  66.6 2.7 %copy-start = (f32[64,2560]{1,0:T(8,128)S(1)}, f32[64,2560]{1,0:T(8,128)}, u32[]{:S(2)}) copy-start(f32[64,2560]{1,0:T(8,128)} %get-tuple-element.5) | copy-start | bytes 1966084

commit v3 on v2

--- a/solution.py
+++ b/solution.py
@@ -92,11 +92,13 @@
 def kernel(
     wind, offs, ratio, magic, screens, amp_h, dcol_h, drow_h,
     new_out, spots,
-    x, amp, dcol, drow, send1, recv_a, recv_b, recv_c, halo_s, halo_r, edge_s, edge_r, y,
-    relb, frac, b_a, b_b, b_c, send2a, send2b, recv2a, recv2b, wbig_a, wbig_b, ampn, phase, field,
-    in_sem, tab_sem, s1, r1, hs, hr, es, er, ws, wr, s2, r2, osem,
+    x, amp, dcol, drow, send1, recv_a, recv_b, recv_c, side_s, side_r, edge_s, edge_r, y,
+    relb, frac, cols, mate_a, mate_b, mate_c, rows_a, rows_b, rows_c, kidx,
+    send2a, send2b, recv2a, recv2b, wbig_a, wbig_b, ampn, phase, field,
+    in_sem, tab_sem, s1, r1, hs, hr, ws, wr, s2, r2, osem,
 ):
-    recv1, cols = (recv_a, recv_b, recv_c), (b_a, b_b, b_c)
+    recv1 = (recv_a, recv_b, recv_c)
+    mate, rows = (mate_a, mate_b, mate_c), (rows_a, rows_b, rows_c)
     b = lax.axis_index("layer")
     q = lax.axis_index("dir")
     xl, c = q // 2, q % 2
@@ -105,13 +107,13 @@
     def device(pb, pxl):
         return (pb, pxl * 2 + c)
 
-    up = (b, (q + 1) % 4)
-    down = (b, (q + 3) % 4)
-    right = ((b + 1) % 32, q)
-    left = ((b + 31) % 32, q)
+    def block(db, dq):
+        return ((b + db) & 31, (q + dq) & 3)
+
+    near = [(db, dq) for db in (-1, 0, 1) for dq in (-1, 1)]
     bar = pltpu.get_barrier_semaphore()
-    for dev in (up, down):
-        pl.semaphore_signal(bar, inc=1, device_id=dev, device_id_type=MESH)
+    for n in near:
+        pl.semaphore_signal(bar, inc=1, device_id=block(*n), device_id_type=MESH)
 
     def greet(k, _):
         pl.semaphore_signal(bar, inc=1, device_id=device(*shift_at(b, xl, 64 - k)), device_id_type=MESH)
@@ -132,9 +134,9 @@
 
     def permute(l):
         loads[l].wait()
-        rows = jnp.dot(perm, x[l], preferred_element_type=F32)
+        ordered = jnp.dot(perm, x[l], preferred_element_type=F32)
         for t in range(4):
-            send1[l, :, t] = rows[:, t * 128:(t + 1) * 128].reshape(CHIPS, 8, 128).astype(BF16)
+            send1[l, :, t] = ordered[:, t * 128:(t + 1) * 128].reshape(CHIPS, 8, 128).astype(BF16)
 
     def exchange(l):
         def go(k, _):
@@ -150,31 +152,56 @@
         lax.fori_loop(1, CHIPS, go, 0)
         pltpu.make_async_copy(send1.at[l, chip], recv1[l].at[xl, pl.ds(b * 4, 4)], r1.at[l]).start()
 
+    def sent(l):
+        pltpu.make_async_copy(send1.at[l, 0:63], send1.at[l, 0:63], s1.at[l]).wait()
+
     permute(0)
-    pl.semaphore_wait(bar, 65)
+    pl.semaphore_wait(bar, 63 + len(near))
     exchange(0)
     permute(1)
-    exchange(1)
     permute(2)
-    exchange(2)
 
     lane8, row8 = iota((8, 128), 1), iota((8, 128), 0)
     first = jnp.where(lane8 == row8, 1.0, 0.0).astype(BF16)
     last = jnp.where(lane8 == row8 + 120, 1.0, 0.0).astype(BF16)
     nt = (((1,), (1,)), ((), ()))
     for l in range(LAYERS):
-        halo_s[0, l] = lax.dot_general(
+        side_s[0, l] = lax.dot_general(
             last, x[l, :, BLK - 128:], nt, preferred_element_type=F32).astype(BF16)
-        halo_s[1, l] = lax.dot_general(
+        side_s[1, l] = lax.dot_general(
             first, x[l, :, :128], nt, preferred_element_type=F32).astype(BF16)
-    halos = [
-        pltpu.make_async_remote_copy(
-            src_ref=halo_s.at[i], dst_ref=halo_r.at[i], send_sem=hs.at[i], recv_sem=hr.at[i],
-            device_id=dev, device_id_type=MESH)
-        for i, dev in enumerate((right, left))
-    ]
+        edge_s[0, l] = x[l, BLK - 8:]
+        edge_s[1, l] = x[l, :8]
+
+    def halo(i, src, dst, to):
+        return pltpu.make_async_remote_copy(
+            src_ref=src, dst_ref=dst, send_sem=hs.at[i], recv_sem=hr.at[i],
+            device_id=to, device_id_type=MESH)
+
+    halos = []
+    for i, db in enumerate((1, -1)):
+        dst = side_r.at[i]
+        halos.append(halo(4 * i, side_s.at[i], dst.at[:, :, 128:128 + BLK], block(db, 0)))
+        halos.append(halo(4 * i + 1, side_s.at[i, :, :, BLK - 128:], dst.at[:, :, :128], block(db, 1)))
+        halos.append(halo(4 * i + 2, side_s.at[i, :, :, :128], dst.at[:, :, 128 + BLK:], block(db, -1)))
+        halos.append(halo(4 * i + 3, edge_s.at[i], edge_r.at[i], block(0, db)))
     for h in halos:
         h.start()
+
+    sent(0)
+    exchange(1)
+
+    def row_table(p, _):
+        for l in range(LAYERS):
+            for pxl in range(2):
+                d = pxl * 2 + c
+                num, den = ratio[l, 0, d], ratio[l, 1, d]
+                r = offs[l, 0, d] - wind[0, l] + ROWS + stretch(p, NPR, num, den, magic[den])
+                kidx[l, p * 2 + pxl] = ((r + ((chip - r) & 63)) & (ROWS - 1)) >> 6
+        return 0
+
+    lax.fori_loop(0, 32, row_table, 0)
+    cols[...] = jnp.zeros_like(cols)
 
     px0 = (iota((16, 128), 0) * 128).astype(F32)
     px = px0 + iota((16, 128), 1).astype(F32)
@@ -224,51 +251,38 @@
         energy = jnp.dot(energy, g128, precision=HIGHEST, preferred_element_type=F32)
         ampn[j] = av / jnp.sqrt(energy)
 
+    sent(1)
+    exchange(2)
     for h in halos:
         h.wait()
     tn = (((0,), (0,)), ((), ()))
-    lane = iota((BLK, 128), 1)
     for l in range(LAYERS):
-        w1 = wind[1, l]
-        lanes = [lax.dot_general(halo_r[0, l], last, tn, preferred_element_type=F32)]
-        lanes += [x[l, :, t * 128:(t + 1) * 128].astype(F32) for t in range(4)]
-        lanes += [lax.dot_general(halo_r[1, l], first, tn, preferred_element_type=F32)]
-        turned = [pltpu.roll(v, (w1 + 128) & 127, 1) for v in lanes]
-        before, after = lane < w1, lane >= 128 + w1
+        w0, w1 = wind[0, l], wind[1, l]
+        left = lax.dot_general(side_r[0, l], last, tn, preferred_element_type=F32)
+        right = lax.dot_general(side_r[1, l], first, tn, preferred_element_type=F32)
+        for r0, n, src in ((0, 8, edge_r.at[0, l]), (8, BLK, x.at[l]), (BLK + 8, 8, edge_r.at[1, l])):
+            at = r0 + 120
+            lanes = [left[at:at + n]]
+            lanes += [src[:, t * 128:(t + 1) * 128].astype(F32) for t in range(4)]
+            lanes += [right[at:at + n]]
+            turned = [pltpu.roll(v, (w1 + 128) & 127, 1) for v in lanes]
+            lane = iota((n, 128), 1)
+            before, after = lane < w1, lane >= 128 + w1
+            for t in range(4):
+                y[r0:r0 + n, t * 128:(t + 1) * 128] = jnp.where(
+                    before, turned[t], jnp.where(after, turned[t + 2], turned[t + 1]))
+        turn, whole = w0 & 7, w0 >> 3
+        keep = iota((BLK // 8 + 1, 8, 128), 1) >= turn
         for t in range(4):
-            val = jnp.where(before, turned[t], jnp.where(after, turned[t + 2], turned[t + 1]))
-            y[l, 8:8 + BLK, t * 128:(t + 1) * 128] = val
-        edge_s[0, l] = y[l, BLK:BLK + 8].astype(BF16)
-        edge_s[1, l] = y[l, 8:16].astype(BF16)
-    edges = [
-        pltpu.make_async_remote_copy(
-            src_ref=edge_s.at[i], dst_ref=edge_r.at[i], send_sem=es.at[i], recv_sem=er.at[i],
-            device_id=dev, device_id_type=MESH)
-        for i, dev in enumerate((up, down))
-    ]
-    for e in edges:
-        e.start()
-
-    def flow_rows():
-        for e in edges:
-            e.wait()
-        for l in range(LAYERS):
-            y[l, 0:8] = edge_r[0, l].astype(F32)
-            y[l, BLK + 8:BLK + 16] = edge_r[1, l].astype(F32)
-            w0 = wind[0, l]
-            turn, whole = w0 & 7, w0 >> 3
-            keep = iota((BLK // 8 + 1, 8, 128), 1) >= turn
-            for t in range(4):
-                part = y[l, :, t * 128:(t + 1) * 128].reshape(BLK // 8 + 2, 8, 128)
-                part = pltpu.roll(part, turn, 1)
-                part = jnp.concatenate([part[:1], jnp.where(keep, part[1:], part[:-1])], axis=0)
-                val = jnp.where(whole > 0, part[:-2], jnp.where(whole == 0, part[1:-1], part[2:]))
-                x[l, :, t * 128:(t + 1) * 128] = val.reshape(BLK, 128).astype(BF16)
-            pltpu.make_async_copy(x.at[l], new_out.at[l], osem.at[l]).start()
+            part = y[:, t * 128:(t + 1) * 128].reshape(BLK // 8 + 2, 8, 128)
+            part = pltpu.roll(part, turn, 1)
+            part = jnp.concatenate([part[:1], jnp.where(keep, part[1:], part[:-1])], axis=0)
+            val = jnp.where(whole > 0, part[:-2], jnp.where(whole == 0, part[1:-1], part[2:]))
+            x[l, :, t * 128:(t + 1) * 128] = val.reshape(BLK, 128).astype(BF16)
+        pltpu.make_async_copy(x.at[l], new_out.at[l], osem.at[l]).start()
 
     def columns(l):
-        def one(i, _):
-            d, j = i // JT, i % JT
+        def one(d, j):
             num, den = ratio[l, 0, d], ratio[l, 1, d]
             start = (offs[l, 1, d] - wind[1, l] + COLS) & (COLS - 1)
             tile = (start + stretch(j, 128, num, den, magic[den])) >> 7
@@ -287,14 +301,20 @@
                 vb = jnp.where(sel == 0, g[0], jnp.where(sel == 1, g[1], g[2]))
                 vu = jnp.where(sel_u == 0, u[0], jnp.where(sel_u == 1, u[1], u[2]))
                 out = low * vb + high * vu
-                cols[l].at[d % 2, c, d // 2, h].reshape(128, 128)[pl.ds(j, 8, stride=16), :] = out
+                cols.at[d % 2, d // 2, h].reshape(128, 128)[pl.ds(j, 8, stride=16), :] = out
+
+        def direction(d, _):
+            for j in range(JT):
+                one(d, j)
             return 0
 
-        lax.fori_loop(0, DIRS * JT, one, 0)
+        lax.fori_loop(0, DIRS, direction, 0)
+        mate[l][...] = cols[1 - c].astype(BF16)
+        rows[l][c] = cols[c].astype(BF16)
 
     def swap(l):
         return pltpu.make_async_remote_copy(
-            src_ref=cols[l].at[1 - c, c], dst_ref=cols[l].at[1 - c, c],
+            src_ref=mate[l], dst_ref=rows[l].at[c],
             send_sem=ws.at[l], recv_sem=wr.at[l],
             device_id=(b, xl * 2 + 1 - c), device_id_type=MESH)
 
@@ -303,59 +323,48 @@
         columns(l)
         swap(l).start()
 
-    def row_of(l, p, pxl):
-        d = pxl * 2 + c
-        num, den = ratio[l, 0, d], ratio[l, 1, d]
-        s = offs[l, 0, d] - wind[0, l] + ROWS + stretch(p, NPR, num, den, magic[den])
-        k = ((s + ((chip - s) & 63)) & (ROWS - 1)) >> 6
-        val = cols[l][c, (k >> 3) & 1, pxl, k >> 4, k & 7]
-        return val[:8], val[8:]
+    def row_of(l, dest):
+        k = kidx[l, dest]
+        return rows[l][(k >> 3) & 1, dest & 1, k >> 4, k & 7]
 
     sub = iota((8, 128), 0)
 
-    def deliver(src, dst, i, k, pb, pxl):
-        @pl.when(k > 0)
-        def _():
-            pltpu.make_async_remote_copy(
-                src_ref=src.at[pb * 2 + pxl], dst_ref=dst.at[chip],
-                send_sem=s2.at[i], recv_sem=r2.at[i],
-                device_id=device(pb, pxl), device_id_type=MESH,
-            ).start()
-
-        @pl.when(k == 0)
-        def _():
-            pltpu.make_async_copy(src.at[chip], dst.at[chip], r2.at[i]).start()
-
-    def send_a(i, _):
-        k = 63 - i
-        pb, pxl = shift_at(b, xl, k)
-        a0, a1 = row_of(0, pb, pxl)
-        b0, b1 = row_of(1, pb, pxl)
-        b0, b1 = pltpu.roll(b0, 2, 0), pltpu.roll(b1, 2, 0)
-        send2a[pb * 2 + pxl, 0] = a0.astype(BF16)
-        send2a[pb * 2 + pxl, 1] = jnp.where(sub < 2, a1, b0).astype(BF16)
-        send2a[pb * 2 + pxl, 2] = jnp.where(sub < 2, b0, jnp.where(sub < 4, b1, 0.0)).astype(BF16)
-        deliver(send2a, recv2a, 0, k, pb, pxl)
-        return 0
-
-    def send_b(i, _):
-        k = 63 - i
-        pb, pxl = shift_at(b, xl, k)
-        a0, a1 = row_of(2, pb, pxl)
-        send2b[pb * 2 + pxl, 0] = a0.astype(BF16)
-        send2b[pb * 2 + pxl, 1] = jnp.where(sub < 2, a1, 0.0).astype(BF16)
-        deliver(send2b, recv2b, 1, k, pb, pxl)
-        return 0
+    def pack_a(dest):
+        val_a, val_b = row_of(0, dest).astype(F32), row_of(1, dest).astype(F32)
+        b0, b1 = pltpu.roll(val_b[:8], 2, 0), pltpu.roll(val_b[8:], 2, 0)
+        send2a[dest, 0] = val_a[:8].astype(BF16)
+        send2a[dest, 1] = jnp.where(sub < 2, val_a[8:], b0).astype(BF16)
+        send2a[dest, 2] = jnp.where(sub < 2, b0, b1).astype(BF16)
+
+    def pack_b(dest):
+        send2b[dest] = row_of(2, dest)
+
+    def deliver(i, src, dst, pack):
+        def some(n, _):
+            for u in range(7):
+                pb, pxl = shift_at(b, xl, 63 - n * 7 - u)
+                pack(pb * 2 + pxl)
+            for u in range(7):
+                pb, pxl = shift_at(b, xl, 63 - n * 7 - u)
+                pltpu.make_async_remote_copy(
+                    src_ref=src.at[pb * 2 + pxl], dst_ref=dst.at[chip],
+                    send_sem=s2.at[i], recv_sem=r2.at[i],
+                    device_id=device(pb, pxl), device_id_type=MESH,
+                ).start()
+            return 0
+
+        lax.fori_loop(0, 9, some, 0)
+        pack(chip)
+        pltpu.make_async_copy(src.at[chip], dst.at[chip], r2.at[i]).start()
 
     arrive(0)
-    flow_rows()
     arrive(1)
     swap(0).wait()
     swap(1).wait()
-    lax.fori_loop(0, CHIPS, send_a, 0)
+    deliver(0, send2a, recv2a, pack_a)
     arrive(2)
     swap(2).wait()
-    lax.fori_loop(0, CHIPS, send_b, 0)
+    deliver(1, send2b, recv2b, pack_b)
 
     pltpu.make_async_copy(recv2a, recv2a, r2.at[0]).wait()
     phase[...] = jnp.dot(
@@ -377,8 +386,8 @@
         spots[:, j * 256:(j + 1) * 256] = full[:64] * full[:64] + full[64:] * full[64:]
 
     for l in range(LAYERS):
-        pltpu.make_async_copy(send1.at[l, 0:63], send1.at[l, 0:63], s1.at[l]).wait()
         pltpu.make_async_copy(x.at[l], new_out.at[l], osem.at[l]).wait()
+    sent(2)
     pltpu.make_async_copy(send2a.at[0:63], send2a.at[0:63], s2.at[0]).wait()
     pltpu.make_async_copy(send2b.at[0:63], send2b.at[0:63], s2.at[1]).wait()
 
@@ -407,25 +416,26 @@
             pltpu.VMEM((2, 128, 8, 128), BF16),
             pltpu.VMEM((2, 128, 8, 128), BF16),
             pltpu.VMEM((2, LAYERS, 8, BLK), BF16),
+            pltpu.VMEM((2, LAYERS, 8, BLK + 256), BF16),
             pltpu.VMEM((2, LAYERS, 8, BLK), BF16),
             pltpu.VMEM((2, LAYERS, 8, BLK), BF16),
-            pltpu.VMEM((2, LAYERS, 8, BLK), BF16),
-            pltpu.VMEM((LAYERS, BLK + 16, BLK), F32),
+            pltpu.VMEM((BLK + 16, BLK), F32),
             pltpu.VMEM((DIRS * LAYERS, 16, 128), I32),
             pltpu.VMEM((DIRS * LAYERS, 16, 128), F32),
-            pltpu.VMEM((2, 2, 2, 2, 8, 16, 128), F32),
-            pltpu.VMEM((2, 2, 2, 2, 8, 16, 128), F32),
-            pltpu.VMEM((2, 2, 2, 2, 8, 16, 128), F32),
+            pltpu.VMEM((2, 2, 2, 8, 16, 128), F32),
+            *[pltpu.VMEM((2, 2, 8, 16, 128), BF16)] * 3,
+            *[pltpu.VMEM((2, 2, 2, 8, 16, 128), BF16)] * 3,
+            pltpu.SMEM((LAYERS, CHIPS), I32),
             pltpu.VMEM((CHIPS, 3, 8, 128), BF16),
-            pltpu.VMEM((CHIPS, 2, 8, 128), BF16),
+            pltpu.VMEM((CHIPS, 16, 128), BF16),
             pltpu.VMEM((CHIPS, 3, 8, 128), BF16),
-            pltpu.VMEM((CHIPS, 2, 8, 128), BF16),
+            pltpu.VMEM((CHIPS, 16, 128), BF16),
             pltpu.VMEM((JT * NPR, CHIPS * 24), BF16),
             pltpu.VMEM((JT * NPR, CHIPS * 16), BF16),
             pltpu.VMEM((JT, NPR, 128), F32),
             pltpu.VMEM((JT * NPR, 128), F32),
             pltpu.VMEM((2, JT, NPR, 128), F32),
-            dma((3,)), dma((3,)), dma((3,)), dma((3,)), dma((2,)), dma((2,)), dma((2,)), dma((2,)),
+            dma((3,)), dma((3,)), dma((3,)), dma((3,)), dma((8,)), dma((8,)),
             dma((3,)), dma((3,)), dma((2,)), dma((2,)), dma((3,)),
         ],
         compiler_params=pltpu.CompilerParams(

time: 70.4 us -> 50.2 us (0.71)
  Pallas kernels: 65.9 us -> 45.4 us
    pallas_call x1, Pallas kernels: 65.9 us -> 45.4 us  [per_device(): pl.pallas_call(kernel, out_shape=(jax.ShapeDtypeStruct((LAYERS, BLK, BLK)...]
where the time goes in v3:
time: 50.2 us; the launch traced here: 49.6 us
  Pallas kernels  45.4 us (90%)
  local copies, waits for them, and re-layouts  3.56 us (7%)
  between operations  0.65 us (1%)
    pallas_call x1, Pallas kernels, per_device(): pl.pallas_call(kernel, out_shape=(jax.ShapeDtypeStruct((LAYERS, BLK, BLK)...  45.4 us
    unnamed x4, local copies, waits for them, and re-layouts  3.56 us

profile of v3, /device:TPU:0, one launch (start us, length us, event | category | flops | bytes accessed | tf_op | source)
XLA Modules:
  0.0 49.6 jit_solution(124057324194029884)
XLA Ops:
  0.6 45.4 %screens_to_spots.1 = (bf16[3,512,512]{2,1,0:T(8,128)(2,1)}, f32[64,2560]{1,0:T(8,128)}) custom-call(s32[2,3]{1,0:T(2,128)} %bitcast.7, s32[3,2,4]{2,1,0:T(2,128)} %bitcast.5, s32[3,2,4]{2,1,0:T(2,128)} %bitcast.6, s32[129]{0:T(256)} %constant.6.clone.magic, bf16[3,512,512]{2,1,0:T(8,128)(2,1)} %screens.1, f32[32,1280]{1,0:T(8,128)} %amp_h.1, ...), custom_call_target="tpu_custom_call" | custom-call | tf_op jit(solution)/shard_map/screens_to_spots/pallas_call | solution.py:401
  46.1 0.0 copy-start
  46.1 2.7 %copy.12 = bf16[3,512,512]{2,1,0:T(8,128)(2,1)} copy(bf16[3,512,512]{2,1,0:T(8,128)(2,1)} %get-tuple-element.8) | data formatting | bytes 3145728
  48.8 0.0 copy-done
  48.8 0.8 %copy.13 = f32[1,64,2560]{2,1,0:T(8,128)} copy(f32[1,64,2560]{2,1,0:T(8,128)S(1)} %bitcast.4) | data formatting | bytes 1310720
Async XLA Ops:
  46.1 2.7 %copy-start = (f32[64,2560]{1,0:T(8,128)S(1)}, f32[64,2560]{1,0:T(8,128)}, u32[]{:S(2)}) copy-start(f32[64,2560]{1,0:T(8,128)} %get-tuple-element.5) | copy-start | bytes 1966084

commit v4 on v3

--- a/solution.py
+++ b/solution.py
@@ -1,5 +1,6 @@
 import jax
 import jax.numpy as jnp
+import ml_dtypes
 import numpy as np
 from jax import lax
 from jax.experimental import pallas as pl
@@ -79,7 +80,23 @@
     cols = np.concatenate([np.kron(np.eye(8), c.T), np.kron(np.eye(8), s.T)], axis=1)
     cb, sb = np.kron(np.eye(2), c), np.kron(np.eye(2), s)
     rows = np.block([[cb, -sb], [sb, cb]])
-    return cols.astype(np.float32), rows.astype(np.float32)
+    cols_hi, cols_lo = halves(cols)
+    rows_hi, rows_lo = halves(rows)
+    return (
+        np.concatenate([cols_hi, cols_lo, cols_hi], axis=0),
+        np.concatenate([rows_hi, rows_lo, rows_hi], axis=1),
+    )
+
+
+def halves(a):
+    a = a.astype(np.float32)
+    hi = a.astype(ml_dtypes.bfloat16)
+    return hi, (a - hi.astype(np.float32)).astype(ml_dtypes.bfloat16)
+
+
+def split(a):
+    hi = a.astype(BF16)
+    return hi, (a - hi.astype(F32)).astype(BF16)
 
 
 def shift_at(b, xl, k):
@@ -90,11 +107,11 @@
 
 
 def kernel(
-    wind, offs, ratio, magic, screens, amp_h, dcol_h, drow_h,
-    new_out, spots,
-    x, amp, dcol, drow, send1, recv_a, recv_b, recv_c, side_s, side_r, edge_s, edge_r, y,
+    wind, offs, ratio, magic, screens, amp_h,
+    new_out, phase, ampn,
+    x, amp, send1, recv_a, recv_b, recv_c, side_s, side_r, edge_s, edge_r, y,
     relb, frac, cols, mate_a, mate_b, mate_c, rows_a, rows_b, rows_c, kidx,
-    send2a, send2b, recv2a, recv2b, wbig_a, wbig_b, ampn, phase, field,
+    send2a, send2b, recv2a, recv2b, wbig_a, wbig_b,
     in_sem, tab_sem, s1, r1, hs, hr, ws, wr, s2, r2, osem,
 ):
     recv1 = (recv_a, recv_b, recv_c)
@@ -107,6 +124,10 @@
     def device(pb, pxl):
         return (pb, pxl * 2 + c)
 
+    loads = [pltpu.make_async_copy(screens.at[l], x.at[l], in_sem.at[l]) for l in range(LAYERS)]
+    for load in loads:
+        load.start()
+
     def block(db, dq):
         return ((b + db) & 31, (q + dq) & 3)
 
@@ -121,13 +142,8 @@
 
     lax.fori_loop(1, CHIPS, greet, 0)
 
-    loads = [pltpu.make_async_copy(screens.at[l], x.at[l], in_sem.at[l]) for l in range(LAYERS)]
-    tables = [
-        pltpu.make_async_copy(src, dst, tab_sem.at[i])
-        for i, (src, dst) in enumerate(((amp_h, amp), (dcol_h, dcol), (drow_h, drow)))
-    ]
-    for load in loads + tables:
-        load.start()
+    amp_load = pltpu.make_async_copy(amp_h, amp, tab_sem)
+    amp_load.start()
 
     ro, ri = iota((BLK, BLK), 0), iota((BLK, BLK), 1)
     perm = jnp.where(ri == (ro & 7) * 64 + (ro >> 3), 1.0, 0.0).astype(BF16)
@@ -241,8 +257,7 @@
     for j in range(JT):
         wbig_b[j * NPR:(j + 1) * NPR] = jnp.where((cb & 15) == j, wb, 0.0).astype(BF16)
 
-    for load in tables:
-        load.wait()
+    amp_load.wait()
     g32 = jnp.where((iota((32, 32), 0) >> 4) == (iota((32, 32), 1) >> 4), 1.0, 0.0)
     g128 = jnp.where((iota((128, 128), 0) >> 4) == (iota((128, 128), 1) >> 4), 1.0, 0.0)
     for j in range(JT):
@@ -372,18 +387,6 @@
     pltpu.make_async_copy(recv2b, recv2b, r2.at[1]).wait()
     phase[...] += jnp.dot(
         wbig_b[...], recv2b[...].reshape(CHIPS * 16, 128), preferred_element_type=F32)
-    for j in range(JT):
-        sin, cos = sincos(phase[j * NPR:(j + 1) * NPR])
-        field[0, j] = ampn[j] * cos
-        field[1, j] = ampn[j] * sin
-    for j in range(JT):
-        both = jnp.concatenate([field[0, j], field[1, j]], axis=0)
-        g = jnp.dot(both, dcol[...], precision=HIGHEST, preferred_element_type=F32)
-        half_re = g[:32, :256] - g[32:, 256:]
-        half_im = g[:32, 256:] + g[32:, :256]
-        half = jnp.concatenate([half_re, half_im], axis=0)
-        full = jnp.dot(drow[...], half, precision=HIGHEST, preferred_element_type=F32)
-        spots[:, j * 256:(j + 1) * 256] = full[:64] * full[:64] + full[64:] * full[64:]
 
     for l in range(LAYERS):
         pltpu.make_async_copy(x.at[l], new_out.at[l], osem.at[l]).wait()
@@ -392,25 +395,54 @@
     pltpu.make_async_copy(send2b.at[0:63], send2b.at[0:63], s2.at[1]).wait()
 
 
+def image(phase, ampn, dcol, drow, new_in, new_out, spots, field, half, out, nsem, osem):
+    copy = pltpu.make_async_copy(new_in, new_out, nsem)
+    copy.start()
+    for j in range(JT):
+        sin, cos = sincos(phase[j * NPR:(j + 1) * NPR])
+        for i, v in enumerate((ampn[j] * cos, ampn[j] * sin)):
+            hi, lo = split(v)
+            at = j * 64 + i * 32
+            field[at:at + 32, :128] = hi
+            field[at:at + 32, 128:256] = hi
+            field[at:at + 32, 256:] = lo
+    half[...] = jnp.dot(field[...], dcol[...], preferred_element_type=F32)
+    stores = []
+    for j in range(JT):
+        g = half[j * 64:(j + 1) * 64]
+        re = split(g[:32, :256] - g[32:, 256:])
+        im = split(g[:32, 256:] + g[32:, :256])
+        data = jnp.concatenate([re[0], im[0], re[0], im[0], re[1], im[1]], axis=0)
+        full = jnp.dot(drow[...], data, preferred_element_type=F32)
+        out[:, j * 256:(j + 1) * 256] = full[:64] * full[:64] + full[64:] * full[64:]
+        store = pltpu.make_async_copy(
+            out.at[:, j * 256:(j + 1) * 256], spots.at[:, j * 256:(j + 1) * 256], osem.at[j])
+        store.start()
+        stores.append(store)
+    for store in stores:
+        store.wait()
+    copy.wait()
+
+
 def per_device(screens, amplitude, wind, offsets, ratio):
-    cols, rows = dft_tables()
+    dcol, drow = dft_tables()
     vmem = pl.BlockSpec(memory_space=pltpu.VMEM)
     smem = pl.BlockSpec(memory_space=pltpu.SMEM)
-    hbm = pl.BlockSpec(memory_space=pl.ANY)
+    hbm = pl.BlockSpec(memory_space=pltpu.HBM)
+    anywhere = pl.BlockSpec(memory_space=pl.ANY)
     dma = pltpu.SemaphoreType.DMA
-    new, spots = pl.pallas_call(
+    new, phase, ampn = pl.pallas_call(
         kernel,
         out_shape=(
             jax.ShapeDtypeStruct((LAYERS, BLK, BLK), BF16),
-            jax.ShapeDtypeStruct((64, 2560), F32),
+            jax.ShapeDtypeStruct((JT * NPR, 128), F32),
+            jax.ShapeDtypeStruct((JT, NPR, 128), F32),
         ),
-        in_specs=[smem, smem, smem, smem, hbm, hbm, hbm, hbm],
-        out_specs=(hbm, vmem),
+        in_specs=[smem, smem, smem, smem, hbm, hbm],
+        out_specs=(anywhere, vmem, vmem),
         scratch_shapes=[
             pltpu.VMEM((LAYERS, BLK, BLK), BF16),
             pltpu.VMEM((NPR, PC), F32),
-            pltpu.VMEM((128, 512), F32),
-            pltpu.VMEM((128, 64), F32),
             pltpu.VMEM((LAYERS, CHIPS, 4, 8, 128), BF16),
             pltpu.VMEM((2, 128, 8, 128), BF16),
             pltpu.VMEM((2, 128, 8, 128), BF16),
@@ -432,16 +464,38 @@
             pltpu.VMEM((CHIPS, 16, 128), BF16),
             pltpu.VMEM((JT * NPR, CHIPS * 24), BF16),
             pltpu.VMEM((JT * NPR, CHIPS * 16), BF16),
-            pltpu.VMEM((JT, NPR, 128), F32),
-            pltpu.VMEM((JT * NPR, 128), F32),
-            pltpu.VMEM((2, JT, NPR, 128), F32),
-            dma((3,)), dma((3,)), dma((3,)), dma((3,)), dma((8,)), dma((8,)),
+            dma((3,)), dma, dma((3,)), dma((3,)), dma((8,)), dma((8,)),
             dma((3,)), dma((3,)), dma((2,)), dma((2,)), dma((3,)),
         ],
         compiler_params=pltpu.CompilerParams(
-            collective_id=0, has_side_effects=True, vmem_limit_bytes=63 << 20),
-        name="screens_to_spots",
-    )(wind.T, offsets.transpose(1, 2, 0), ratio.transpose(1, 2, 0), jnp.asarray(reciprocals()), screens, amplitude, jnp.asarray(cols), jnp.asarray(rows))
+            collective_id=0, has_side_effects=True, vmem_limit_bytes=32 << 20),
+        name="screens_to_phase",
+    )(
+        *[
+            pltpu.with_memory_space_constraint(v, pltpu.HBM)
+            for v in (
+                wind.T, offsets.transpose(1, 2, 0), ratio.transpose(1, 2, 0),
+                jnp.asarray(reciprocals()), screens, amplitude,
+            )
+        ]
+    )
+    new, spots = pl.pallas_call(
+        image,
+        out_shape=(
+            jax.ShapeDtypeStruct((LAYERS, BLK, BLK), BF16),
+            jax.ShapeDtypeStruct((64, 2560), F32),
+        ),
+        in_specs=[vmem, vmem, vmem, vmem, anywhere],
+        out_specs=(hbm, hbm),
+        scratch_shapes=[
+            pltpu.VMEM((JT * 64, 384), BF16),
+            pltpu.VMEM((JT * 64, 512), F32),
+            pltpu.VMEM((64, 2560), F32),
+            dma, dma((JT,)),
+        ],
+        compiler_params=pltpu.CompilerParams(vmem_limit_bytes=32 << 20),
+        name="phase_to_spots",
+    )(phase, ampn, jnp.asarray(dcol), jnp.asarray(drow), new)
     return new, spots[None]
 
 

time: 50.2 us -> 44.9 us (0.89)
  local copies, waits for them, and re-layouts: 3.56 us -> 0.01 us
  Pallas kernels: 45.4 us -> 43.8 us
    pallas_call x1, Pallas kernels: 45.4 us -> 41.8 us  [per_device(): pl.pallas_call(kernel, out_shape=(jax.ShapeDtypeStruct((LAYERS, BLK, BLK)...]
    unnamed x4, local copies, waits for them, and re-layouts: 3.56 us -> 0.01 us
    pallas_call x0 -> x1, Pallas kernels: none -> 1.92 us  [per_device(): pl.pallas_call(image, out_shape=(jax.ShapeDtypeStruct((LAYERS, BLK, BLK),...]
where the time goes in v4:
time: 44.9 us; the launch traced here: 44.4 us
  Pallas kernels  43.8 us (98%)
  between operations  0.67 us (1%)
    pallas_call x1, Pallas kernels, per_device(): pl.pallas_call(kernel, out_shape=(jax.ShapeDtypeStruct((LAYERS, BLK, BLK)...  41.8 us
    pallas_call x1, Pallas kernels, per_device(): pl.pallas_call(image, out_shape=(jax.ShapeDtypeStruct((LAYERS, BLK, BLK),...  1.92 us

profile of v4, /device:TPU:0, one launch (start us, length us, event | category | flops | bytes accessed | tf_op | source)
XLA Modules:
  0.0 44.4 jit_solution(2466925286034071748)
XLA Ops:
  0.6 0.0 copy-start.1
  0.6 0.0 copy-start
  0.7 41.8 %screens_to_phase.1 = (bf16[3,512,512]{2,1,0:T(8,128)(2,1)S(1)}, f32[320,128]{1,0:T(8,128)S(1)}, f32[10,32,128]{2,1,0:T(8,128)S(1)}) custom-call(s32[2,3]{1,0:T(2,128)} %bitcast.6, s32[3,2,4]{2,1,0:T(2,128)} %bitcast.4, s32[3,2,4]{2,1,0:T(2,128)} %bitcast.5, s32[129]{0:T(256)} %constant.6.clone.magic, bf16[3,512,512]{2,1,0:T(8,128)(2,1)} %screens.1, ...), custom_call_target="tpu_custom_call" | custom-call | tf_op jit(solution)/shard_map/screens_to_phase/pallas_call | solution.py:434
  42.5 0.0 copy-done.1
  42.5 0.0 copy-done
  42.5 1.9 %phase_to_spots.1 = (bf16[3,512,512]{2,1,0:T(8,128)(2,1)}, f32[64,2560]{1,0:T(8,128)}) custom-call(f32[320,128]{1,0:T(8,128)S(1)} %get-tuple-element.7.phase, f32[10,32,128]{2,1,0:T(8,128)S(1)} %get-tuple-element.8.ampn, bf16[384,512]{1,0:T(8,128)(2,1)S(1)} %copy-done, bf16[128,192]{1,0:T(8,128)(2,1)S(1)} %copy-done.1, ...), custom_call_target="tpu_custom_call" | custom-call | tf_op jit(solution)/shard_map/phase_to_spots/pallas_call | solution.py:482
Async XLA Ops:
  0.6 41.9 %copy-start.1 = (bf16[128,192]{1,0:T(8,128)(2,1)S(1)}, bf16[128,192]{1,0:T(8,128)(2,1)}, u32[]{:S(2)}) copy-start(bf16[128,192]{1,0:T(8,128)(2,1)} %constant.8.clone.drow) | copy-start | bytes 147460
  0.6 41.9 %copy-start = (bf16[384,512]{1,0:T(8,128)(2,1)S(1)}, bf16[384,512]{1,0:T(8,128)(2,1)}, u32[]{:S(2)}) copy-start(bf16[384,512]{1,0:T(8,128)(2,1)} %constant.7.clone.dcol) | copy-start | bytes 1179652

commit v5 on v4

--- a/solution.py
+++ b/solution.py
@@ -246,16 +246,18 @@
         low = (1.0 - f).astype(BF16).astype(F32)
         return jnp.where(mrow == base, low, 0.0) + jnp.where(mrow == ((base + 1) & 63), high, 0.0)
 
-    ca = iota((NPR, CHIPS * 24), 1)
-    ma = (ca * 2731) >> 16
-    ja = ca - ma * 24
-    wa = jnp.where(ja < 10, row_weights(0, ma), row_weights(1, ma))
+    cc = iota((NPR, CHIPS * 16), 1)
+    m, r = cc >> 4, cc & 15
+    w0, w1, w2 = [row_weights(l, m) for l in range(LAYERS)]
+    wa, wb = jnp.where(r < 10, w0, w1), jnp.where(r < 4, w1, w2)
     for j in range(JT):
-        wbig_a[j * NPR:(j + 1) * NPR] = jnp.where((ja == j) | (ja == j + 10), wa, 0.0).astype(BF16)
-    cb = iota((NPR, CHIPS * 16), 1)
-    wb = row_weights(2, cb >> 4)
-    for j in range(JT):
-        wbig_b[j * NPR:(j + 1) * NPR] = jnp.where((cb & 15) == j, wb, 0.0).astype(BF16)
+        in_a, in_b = r == j, (r == j + 4) & (r >= 4)
+        if j < 6:
+            in_a = in_a | (r == j + 10)
+        else:
+            in_b = in_b | (r == j - 6)
+        wbig_a[j * NPR:(j + 1) * NPR] = jnp.where(in_a, wa, 0.0).astype(BF16)
+        wbig_b[j * NPR:(j + 1) * NPR] = jnp.where(in_b, wb, 0.0).astype(BF16)
 
     amp_load.wait()
     g32 = jnp.where((iota((32, 32), 0) >> 4) == (iota((32, 32), 1) >> 4), 1.0, 0.0)
@@ -344,15 +346,19 @@
 
     sub = iota((8, 128), 0)
 
+    def turn_rows(v, n):
+        return pltpu.roll(v[:8], n, 0), pltpu.roll(v[8:], n, 0)
+
     def pack_a(dest):
-        val_a, val_b = row_of(0, dest).astype(F32), row_of(1, dest).astype(F32)
-        b0, b1 = pltpu.roll(val_b[:8], 2, 0), pltpu.roll(val_b[8:], 2, 0)
-        send2a[dest, 0] = val_a[:8].astype(BF16)
-        send2a[dest, 1] = jnp.where(sub < 2, val_a[8:], b0).astype(BF16)
-        send2a[dest, 2] = jnp.where(sub < 2, b0, b1).astype(BF16)
+        a, b0 = row_of(0, dest).astype(F32), row_of(1, dest).astype(F32)
+        t0, _ = turn_rows(b0, 2)
+        send2a[dest] = jnp.concatenate([a[:8], jnp.where(sub < 2, a[8:], t0)], axis=0).astype(BF16)
 
     def pack_b(dest):
-        send2b[dest] = row_of(2, dest)
+        t0, t1 = turn_rows(row_of(1, dest).astype(F32), 2)
+        u0, u1 = turn_rows(row_of(2, dest).astype(F32), 4)
+        top = jnp.where(sub < 2, t0, jnp.where(sub < 4, t1, u0))
+        send2b[dest] = jnp.concatenate([top, jnp.where(sub < 4, u0, u1)], axis=0).astype(BF16)
 
     def deliver(i, src, dst, pack):
         def some(n, _):
@@ -383,7 +389,7 @@
 
     pltpu.make_async_copy(recv2a, recv2a, r2.at[0]).wait()
     phase[...] = jnp.dot(
-        wbig_a[...], recv2a[...].reshape(CHIPS * 24, 128), preferred_element_type=F32)
+        wbig_a[...], recv2a[...].reshape(CHIPS * 16, 128), preferred_element_type=F32)
     pltpu.make_async_copy(recv2b, recv2b, r2.at[1]).wait()
     phase[...] += jnp.dot(
         wbig_b[...], recv2b[...].reshape(CHIPS * 16, 128), preferred_element_type=F32)
@@ -458,11 +464,11 @@
             *[pltpu.VMEM((2, 2, 8, 16, 128), BF16)] * 3,
             *[pltpu.VMEM((2, 2, 2, 8, 16, 128), BF16)] * 3,
             pltpu.SMEM((LAYERS, CHIPS), I32),
-            pltpu.VMEM((CHIPS, 3, 8, 128), BF16),
             pltpu.VMEM((CHIPS, 16, 128), BF16),
-            pltpu.VMEM((CHIPS, 3, 8, 128), BF16),
             pltpu.VMEM((CHIPS, 16, 128), BF16),
-            pltpu.VMEM((JT * NPR, CHIPS * 24), BF16),
+            pltpu.VMEM((CHIPS, 16, 128), BF16),
+            pltpu.VMEM((CHIPS, 16, 128), BF16),
+            pltpu.VMEM((JT * NPR, CHIPS * 16), BF16),
             pltpu.VMEM((JT * NPR, CHIPS * 16), BF16),
             dma((3,)), dma, dma((3,)), dma((3,)), dma((8,)), dma((8,)),
             dma((3,)), dma((3,)), dma((2,)), dma((2,)), dma((3,)),

time: 44.9 us -> 45.1 us (level)
  no operation moved by 1% of the time
where the time goes in v5:
time: 45.1 us; the launch traced here: 44.4 us
  Pallas kernels  43.7 us (97%)
  between operations  0.67 us (1%)
    pallas_call x1, Pallas kernels, per_device(): pl.pallas_call(kernel, out_shape=(jax.ShapeDtypeStruct((LAYERS, BLK, BLK)...  41.8 us
    pallas_call x1, Pallas kernels, per_device(): pl.pallas_call(image, out_shape=(jax.ShapeDtypeStruct((LAYERS, BLK, BLK),...  1.92 us

profile of v5, /device:TPU:0, one launch (start us, length us, event | category | flops | bytes accessed | tf_op | source)
XLA Modules:
  0.0 44.4 jit_solution(15316928682445283538)
XLA Ops:
  0.6 0.0 copy-start.1
  0.6 0.0 copy-start
  0.7 41.8 %screens_to_phase.1 = (bf16[3,512,512]{2,1,0:T(8,128)(2,1)S(1)}, f32[320,128]{1,0:T(8,128)S(1)}, f32[10,32,128]{2,1,0:T(8,128)S(1)}) custom-call(s32[2,3]{1,0:T(2,128)} %bitcast.6, s32[3,2,4]{2,1,0:T(2,128)} %bitcast.4, s32[3,2,4]{2,1,0:T(2,128)} %bitcast.5, s32[129]{0:T(256)} %constant.6.clone.magic, bf16[3,512,512]{2,1,0:T(8,128)(2,1)} %screens.1, ...), custom_call_target="tpu_custom_call" | custom-call | tf_op jit(solution)/shard_map/screens_to_phase/pallas_call | solution.py:440
  42.5 0.0 copy-done.1
  42.5 0.0 copy-done
  42.5 1.9 %phase_to_spots.1 = (bf16[3,512,512]{2,1,0:T(8,128)(2,1)}, f32[64,2560]{1,0:T(8,128)}) custom-call(f32[320,128]{1,0:T(8,128)S(1)} %get-tuple-element.7.phase, f32[10,32,128]{2,1,0:T(8,128)S(1)} %get-tuple-element.8.ampn, bf16[384,512]{1,0:T(8,128)(2,1)S(1)} %copy-done, bf16[128,192]{1,0:T(8,128)(2,1)S(1)} %copy-done.1, ...), custom_call_target="tpu_custom_call" | custom-call | tf_op jit(solution)/shard_map/phase_to_spots/pallas_call | solution.py:488
Async XLA Ops:
  0.6 41.9 %copy-start.1 = (bf16[128,192]{1,0:T(8,128)(2,1)S(1)}, bf16[128,192]{1,0:T(8,128)(2,1)}, u32[]{:S(2)}) copy-start(bf16[128,192]{1,0:T(8,128)(2,1)} %constant.8.clone.drow) | copy-start | bytes 147460
  0.6 41.9 %copy-start = (bf16[384,512]{1,0:T(8,128)(2,1)S(1)}, bf16[384,512]{1,0:T(8,128)(2,1)}, u32[]{:S(2)}) copy-start(bf16[384,512]{1,0:T(8,128)(2,1)} %constant.7.clone.dcol) | copy-start | bytes 1179652

commit v6 on v5

--- a/solution.py
+++ b/solution.py
@@ -320,13 +320,18 @@
                 out = low * vb + high * vu
                 cols.at[d % 2, d // 2, h].reshape(128, 128)[pl.ds(j, 8, stride=16), :] = out
 
-        def direction(d, _):
-            for j in range(JT):
-                one(d, j)
-            return 0
-
-        lax.fori_loop(0, DIRS, direction, 0)
+        def toward(core):
+            def direction(i, _):
+                for j in range(JT):
+                    one(2 * i + core, j)
+                return 0
+
+            lax.fori_loop(0, 2, direction, 0)
+
+        toward(1 - c)
         mate[l][...] = cols[1 - c].astype(BF16)
+        swap(l).start()
+        toward(c)
         rows[l][c] = cols[c].astype(BF16)
 
     def swap(l):
@@ -338,7 +343,6 @@
     def arrive(l):
         pltpu.make_async_copy(recv1[l], recv1[l], r1.at[l]).wait()
         columns(l)
-        swap(l).start()
 
     def row_of(l, dest):
         k = kidx[l, dest]
@@ -369,14 +373,14 @@
                 pb, pxl = shift_at(b, xl, 63 - n * 7 - u)
                 pltpu.make_async_remote_copy(
                     src_ref=src.at[pb * 2 + pxl], dst_ref=dst.at[chip],
-                    send_sem=s2.at[i], recv_sem=r2.at[i],
+                    send_sem=s2.at[i], recv_sem=r2.at[i * (1 + (chip >> 4))],
                     device_id=device(pb, pxl), device_id_type=MESH,
                 ).start()
             return 0
 
         lax.fori_loop(0, 9, some, 0)
         pack(chip)
-        pltpu.make_async_copy(src.at[chip], dst.at[chip], r2.at[i]).start()
+        pltpu.make_async_copy(src.at[chip], dst.at[chip], r2.at[i * (1 + (chip >> 4))]).start()
 
     arrive(0)
     arrive(1)
@@ -390,9 +394,13 @@
     pltpu.make_async_copy(recv2a, recv2a, r2.at[0]).wait()
     phase[...] = jnp.dot(
         wbig_a[...], recv2a[...].reshape(CHIPS * 16, 128), preferred_element_type=F32)
-    pltpu.make_async_copy(recv2b, recv2b, r2.at[1]).wait()
-    phase[...] += jnp.dot(
-        wbig_b[...], recv2b[...].reshape(CHIPS * 16, 128), preferred_element_type=F32)
+    total = phase[...]
+    for n in range(4):
+        part = recv2b.at[n * 16:(n + 1) * 16]
+        pltpu.make_async_copy(part, part, r2.at[1 + n]).wait()
+        total = total + jnp.dot(
+            wbig_b[:, n * 256:(n + 1) * 256], part[...].reshape(256, 128), preferred_element_type=F32)
+    phase[...] = total
 
     for l in range(LAYERS):
         pltpu.make_async_copy(x.at[l], new_out.at[l], osem.at[l]).wait()
@@ -471,7 +479,7 @@
             pltpu.VMEM((JT * NPR, CHIPS * 16), BF16),
             pltpu.VMEM((JT * NPR, CHIPS * 16), BF16),
             dma((3,)), dma, dma((3,)), dma((3,)), dma((8,)), dma((8,)),
-            dma((3,)), dma((3,)), dma((2,)), dma((2,)), dma((3,)),
+            dma((3,)), dma((3,)), dma((2,)), dma((5,)), dma((3,)),
         ],
         compiler_params=pltpu.CompilerParams(
             collective_id=0, has_side_effects=True, vmem_limit_bytes=32 << 20),

time: 45.1 us -> 44.4 us (0.984)
  Pallas kernels: 43.7 us -> 43.1 us
    pallas_call x1, Pallas kernels: 41.8 us -> 41.1 us  [per_device(): pl.pallas_call(kernel, out_shape=(jax.ShapeDtypeStruct((LAYERS, BLK, BLK)...]
where the time goes in v6:
time: 44.4 us; the launch traced here: 43.7 us
  Pallas kernels  43.1 us (97%)
  between operations  0.67 us (2%)
    pallas_call x1, Pallas kernels, per_device(): pl.pallas_call(kernel, out_shape=(jax.ShapeDtypeStruct((LAYERS, BLK, BLK)...  41.1 us
    pallas_call x1, Pallas kernels, per_device(): pl.pallas_call(image, out_shape=(jax.ShapeDtypeStruct((LAYERS, BLK, BLK),...  1.92 us

profile of v6, /device:TPU:0, one launch (start us, length us, event | category | flops | bytes accessed | tf_op | source)
XLA Modules:
  0.0 43.7 jit_solution(16280714883373493753)
XLA Ops:
  0.6 0.0 copy-start.1
  0.6 0.0 copy-start
  0.7 41.1 %screens_to_phase.1 = (bf16[3,512,512]{2,1,0:T(8,128)(2,1)S(1)}, f32[320,128]{1,0:T(8,128)S(1)}, f32[10,32,128]{2,1,0:T(8,128)S(1)}) custom-call(s32[2,3]{1,0:T(2,128)} %bitcast.6, s32[3,2,4]{2,1,0:T(2,128)} %bitcast.4, s32[3,2,4]{2,1,0:T(2,128)} %bitcast.5, s32[129]{0:T(256)} %constant.6.clone.magic, bf16[3,512,512]{2,1,0:T(8,128)(2,1)} %screens.1, ...), custom_call_target="tpu_custom_call" | custom-call | tf_op jit(solution)/shard_map/screens_to_phase/pallas_call | solution.py:448
  41.8 0.0 copy-done.1
  41.8 0.0 copy-done
  41.8 1.9 %phase_to_spots.1 = (bf16[3,512,512]{2,1,0:T(8,128)(2,1)}, f32[64,2560]{1,0:T(8,128)}) custom-call(f32[320,128]{1,0:T(8,128)S(1)} %get-tuple-element.7.phase, f32[10,32,128]{2,1,0:T(8,128)S(1)} %get-tuple-element.8.ampn, bf16[384,512]{1,0:T(8,128)(2,1)S(1)} %copy-done, bf16[128,192]{1,0:T(8,128)(2,1)S(1)} %copy-done.1, ...), custom_call_target="tpu_custom_call" | custom-call | tf_op jit(solution)/shard_map/phase_to_spots/pallas_call | solution.py:496
Async XLA Ops:
  0.6 41.2 %copy-start.1 = (bf16[128,192]{1,0:T(8,128)(2,1)S(1)}, bf16[128,192]{1,0:T(8,128)(2,1)}, u32[]{:S(2)}) copy-start(bf16[128,192]{1,0:T(8,128)(2,1)} %constant.8.clone.drow) | copy-start | bytes 147460
  0.6 41.2 %copy-start = (bf16[384,512]{1,0:T(8,128)(2,1)S(1)}, bf16[384,512]{1,0:T(8,128)(2,1)}, u32[]{:S(2)}) copy-start(bf16[384,512]{1,0:T(8,128)(2,1)} %constant.7.clone.dcol) | copy-start | bytes 1179652

commit v7 on v6

--- a/solution.py
+++ b/solution.py
@@ -366,11 +366,11 @@
 
     def deliver(i, src, dst, pack):
         def some(n, _):
-            for u in range(7):
-                pb, pxl = shift_at(b, xl, 63 - n * 7 - u)
+            for u in range(3):
+                pb, pxl = shift_at(b, xl, 63 - n * 3 - u)
                 pack(pb * 2 + pxl)
-            for u in range(7):
-                pb, pxl = shift_at(b, xl, 63 - n * 7 - u)
+            for u in range(3):
+                pb, pxl = shift_at(b, xl, 63 - n * 3 - u)
                 pltpu.make_async_remote_copy(
                     src_ref=src.at[pb * 2 + pxl], dst_ref=dst.at[chip],
                     send_sem=s2.at[i], recv_sem=r2.at[i * (1 + (chip >> 4))],
@@ -378,7 +378,7 @@
                 ).start()
             return 0
 
-        lax.fori_loop(0, 9, some, 0)
+        lax.fori_loop(0, 21, some, 0)
         pack(chip)
         pltpu.make_async_copy(src.at[chip], dst.at[chip], r2.at[i * (1 + (chip >> 4))]).start()
 

time: 44.4 us -> 44.4 us (level)
  no operation moved by 1% of the time
where the time goes in v7:
time: 44.4 us; the launch traced here: 43.8 us
  Pallas kernels  43.1 us (97%)
  between operations  0.67 us (2%)
    pallas_call x1, Pallas kernels, per_device(): pl.pallas_call(kernel, out_shape=(jax.ShapeDtypeStruct((LAYERS, BLK, BLK)...  41.2 us
    pallas_call x1, Pallas kernels, per_device(): pl.pallas_call(image, out_shape=(jax.ShapeDtypeStruct((LAYERS, BLK, BLK),...  1.92 us

profile of v7, /device:TPU:0, one launch (start us, length us, event | category | flops | bytes accessed | tf_op | source)
XLA Modules:
  0.0 43.8 jit_solution(6584540858747048976)
XLA Ops:
  0.6 0.0 copy-start.1
  0.6 0.0 copy-start
  0.7 41.2 %screens_to_phase.1 = (bf16[3,512,512]{2,1,0:T(8,128)(2,1)S(1)}, f32[320,128]{1,0:T(8,128)S(1)}, f32[10,32,128]{2,1,0:T(8,128)S(1)}) custom-call(s32[2,3]{1,0:T(2,128)} %bitcast.6, s32[3,2,4]{2,1,0:T(2,128)} %bitcast.4, s32[3,2,4]{2,1,0:T(2,128)} %bitcast.5, s32[129]{0:T(256)} %constant.6.clone.magic, bf16[3,512,512]{2,1,0:T(8,128)(2,1)} %screens.1, ...), custom_call_target="tpu_custom_call" | custom-call | tf_op jit(solution)/shard_map/screens_to_phase/pallas_call | solution.py:448
  41.8 0.0 copy-done.1
  41.8 0.0 copy-done
  41.9 1.9 %phase_to_spots.1 = (bf16[3,512,512]{2,1,0:T(8,128)(2,1)}, f32[64,2560]{1,0:T(8,128)}) custom-call(f32[320,128]{1,0:T(8,128)S(1)} %get-tuple-element.7.phase, f32[10,32,128]{2,1,0:T(8,128)S(1)} %get-tuple-element.8.ampn, bf16[384,512]{1,0:T(8,128)(2,1)S(1)} %copy-done, bf16[128,192]{1,0:T(8,128)(2,1)S(1)} %copy-done.1, ...), custom_call_target="tpu_custom_call" | custom-call | tf_op jit(solution)/shard_map/phase_to_spots/pallas_call | solution.py:496
Async XLA Ops:
  0.6 41.2 %copy-start.1 = (bf16[128,192]{1,0:T(8,128)(2,1)S(1)}, bf16[128,192]{1,0:T(8,128)(2,1)}, u32[]{:S(2)}) copy-start(bf16[128,192]{1,0:T(8,128)(2,1)} %constant.8.clone.drow) | copy-start | bytes 147460
  0.6 41.2 %copy-start = (bf16[384,512]{1,0:T(8,128)(2,1)S(1)}, bf16[384,512]{1,0:T(8,128)(2,1)}, u32[]{:S(2)}) copy-start(bf16[384,512]{1,0:T(8,128)(2,1)} %constant.7.clone.dcol) | copy-start | bytes 1179652
